TPU v7x, 128 devices: a whole 4x4x4 slice. The times are simulated.
128 devices in a mesh: blk: 32 (over x_hi, z, y), grp: 4 (over x_lo, core).
Axes of the slice: x: 4 (x_hi: 2, x_lo: 2; x = x_hi * 2 + x_lo), y: 4, z: 4, core: 2. Of those that a mesh axis runs over, the one named last changes fastest.
Arguments:
- images: bfloat16 [8192, 1536], P('blk'), may hold values from -100 to 100
- defocus: float32 [8192], P('blk'), may hold values from 1 to 12
- class_id: int32 [8192, 1], P('blk'), may hold values from 0 to 255; in each aligned block of 256 rows (0 to 255, 256 to 511, ...) at most 2 rows name the same one
- rotation_id: int32 [8192], P('blk'), may hold values from 0 to 31
- shift_id: int32 [8192], P('blk'), may hold values from 0 to 8
- references: float32 [4, 64, 1536], P('grp', 'blk'), may hold values from -4 to 4
- owner: int32 [4, 64], P('grp'), may hold values from 0 to 63, as said below
- inv_noise: float32 [24], replicated, may hold values from 0.5 to 2
- prior: float32 [24], replicated, may hold values from 0.5 to 2
Outputs:
- evidence: float32 [8192], P('blk')
- new_refs: float32 [4, 64, 1536], P('grp', 'blk')
Inputs may be any that keep to these rules, and one draw needn't show every extreme that they name: `class_id`: among the particles of one index of blk, no class is assigned to more than 2 particles, and some class to exactly 2. `owner`: each row is a permutation of 0 to 63.
All inputs are finite; a program needn't handle non-finite values.
Results may differ from a plain program's by a relative error of at most 0.0036.
Values sent between devices are 32-bit elements; how exact they have to be, the bound alone decides.
No kernel may reach another device: no remote copies, remote signals or barrier semaphores. Data moves between devices by JAX's collectives and lax.ppermute only.
A program may use at most 64 MiB of HBM per device.

v0:
```python
import math

import jax
import jax.numpy as jnp
from jax import lax
from jax.sharding import PartitionSpec as P

CYCLES = 24
ANGLES = 32
SHIFTS = 9
CL_DEV = 2


def contrast_table(defocus):
    frequency = (jnp.arange(CYCLES, dtype=jnp.float32) + 1.0) / CYCLES
    return -jnp.sin(defocus[:, None] * (frequency * frequency)[None, :] + 0.15)


def phase_tables():
    radius = (jnp.arange(CYCLES, dtype=jnp.float32) + 1.0) / (2.0 * CYCLES)
    bearing = 2.0 * math.pi / ANGLES * jnp.arange(ANGLES, dtype=jnp.float32)
    shift_index = jnp.arange(SHIFTS, dtype=jnp.int32)
    shift_x = (shift_index // 3 - 1).astype(jnp.float32)
    shift_y = (shift_index % 3 - 1).astype(jnp.float32)
    along = (
        shift_x[:, None] * jnp.cos(bearing)[None, :] + shift_y[:, None] * jnp.sin(bearing)[None, :]
    )
    phase = -2.0 * math.pi * radius[None, :, None] * along[:, None, :]
    return (jnp.cos(phase), jnp.sin(phase))


def weigh(images, factor):
    row_total = images.shape[0]
    grid = images.astype(jnp.float32).reshape(row_total, 2, CYCLES, ANGLES)
    return (grid * factor[:, None, :, None]).reshape(row_total, -1).astype(jnp.bfloat16)


def make_templates(ref_block):
    block_rows = ref_block.shape[0]
    grid = ref_block.reshape(block_rows, 2, CYCLES, ANGLES)
    angular = jnp.arange(ANGLES, dtype=jnp.int32)
    turning = (
        angular[:, None, None] == (angular[None, None, :] - angular[None, :, None]) % ANGLES
    ).astype(jnp.float32)
    rotated = jnp.einsum("nqka,arb->nrqkb", grid, turning, precision=lax.Precision.HIGHEST)
    phase_cos, phase_sin = phase_tables()
    rotated_re = rotated[:, :, 0][:, :, None]
    rotated_im = rotated[:, :, 1][:, :, None]
    real_part = phase_cos[None, None] * rotated_re - phase_sin[None, None] * rotated_im
    imag_part = phase_sin[None, None] * rotated_re + phase_cos[None, None] * rotated_im
    stacked = jnp.stack([real_part, imag_part], axis=3)
    return stacked.reshape(block_rows * ANGLES * SHIFTS, -1).astype(jnp.bfloat16)


def score_block(ref_block, weighted, contrast_power, score_scale):
    block_rows = ref_block.shape[0]
    templates = make_templates(ref_block)
    cross = lax.dot_general(
        templates, weighted, (((1,), (1,)), ((), ())), preferred_element_type=jnp.float32
    )
    grid = ref_block.reshape(block_rows, 2, CYCLES, ANGLES)
    power = jnp.sum(grid * grid, axis=(1, 3))
    penalty = jnp.dot(power, contrast_power.T, precision=lax.Precision.HIGHEST)
    logits = (
        cross.reshape(block_rows, ANGLES * SHIFTS, -1) - 0.5 * penalty[:, None, :]
    ) * score_scale
    return logits.reshape(block_rows * ANGLES * SHIFTS, -1)


def target_rows(relative, rotation_id, shift_id):
    inside = (relative >= 0) & (relative < CL_DEV)
    return jnp.where(inside, (relative * ANGLES + rotation_id) * SHIFTS + shift_id, -1)


def update(running, logits, target):
    peak, total, picked = running
    new_peak = jnp.maximum(peak, jnp.max(logits, axis=0))
    total = total * jnp.exp(peak - new_peak) + jnp.sum(jnp.exp(logits - new_peak[None, :]), axis=0)
    row_index = jnp.arange(logits.shape[0], dtype=jnp.int32)
    picked = picked + jnp.sum(jnp.where(row_index[:, None] == target[None, :], logits, 0.0), axis=0)
    return (new_peak, total, picked)


def align_terms(images, contrast, weight, rotation_id, shift_id):
    row_total = images.shape[0]
    phase_cos, phase_sin = phase_tables()
    chosen = (shift_id[:, None] == jnp.arange(SHIFTS, dtype=jnp.int32)[None, :]).astype(jnp.float32)
    cos_rows = jnp.dot(
        chosen, phase_cos.reshape(SHIFTS, -1), precision=lax.Precision.HIGHEST
    ).reshape(row_total, CYCLES, ANGLES)
    sin_rows = jnp.dot(
        chosen, phase_sin.reshape(SHIFTS, -1), precision=lax.Precision.HIGHEST
    ).reshape(row_total, CYCLES, ANGLES)
    grid = images.astype(jnp.float32).reshape(row_total, 2, CYCLES, ANGLES)
    unshift_re = cos_rows * grid[:, 0] + sin_rows * grid[:, 1]
    unshift_im = cos_rows * grid[:, 1] - sin_rows * grid[:, 0]
    unshifted = jnp.stack([unshift_re, unshift_im], axis=1)
    angular = jnp.arange(ANGLES, dtype=jnp.int32)
    turning = (
        angular[None, :, None] == (angular[None, None, :] + rotation_id[:, None, None]) % ANGLES
    ).astype(jnp.float32)
    aligned = jnp.einsum("pqka,pab->pqkb", unshifted, turning, precision=lax.Precision.HIGHEST)
    scaled = weight[:, None] * contrast
    numer_term = (aligned * scaled[:, None, :, None]).reshape(row_total, -1)
    denom_term = weight[:, None] * contrast * contrast
    return (numer_term, denom_term)


def finish(numerator, denominator, prior):
    grid = numerator.reshape(-1, 2, CYCLES, ANGLES)
    return (grid / (denominator + prior[None, :])[:, None, :, None]).reshape(numerator.shape)


def shards(images, defocus, class_id, rotation_id, shift_id, references, owner, inv_noise, prior):
    particle_count = images.shape[0]
    group_classes = owner.shape[1]
    class_total = group_classes * lax.axis_size("grp")
    contrast = contrast_table(defocus)
    contrast_power = contrast * contrast * inv_noise[None, :]
    weighted = weigh(images, contrast * inv_noise[None, :])
    score_scale = 1.0 / math.sqrt(images.shape[1])
    local_class = class_id[:, 0] - lax.axis_index("grp") * group_classes
    member = (local_class >= 0) & (local_class < group_classes)
    initial = (
        jnp.full((particle_count,), -1e30, jnp.float32),
        jnp.zeros((particle_count,), jnp.float32),
        jnp.zeros((particle_count,), jnp.float32),
    )
    running = initial
    shard_piece = lax.all_gather(references, "blk", axis=1, tiled=True)
    blocks = shard_piece[0].reshape(-1, CL_DEV, shard_piece.shape[2])
    firsts = CL_DEV * jnp.arange(blocks.shape[0], dtype=jnp.int32)

    def advance(running_state, entries):
        ref_block, block_first = entries
        logits = score_block(ref_block, weighted, contrast_power, score_scale)
        return (
            update(
                running_state, logits, target_rows(local_class - block_first, rotation_id, shift_id)
            ),
            None,
        )

    running, unused = lax.scan(advance, running, (blocks, firsts))
    peak, total, picked = running
    global_peak = lax.pmax(peak, "grp")
    global_total = lax.psum(total * jnp.exp(peak - global_peak), "grp")
    log_sum = global_peak + jnp.log(global_total)
    log_orients = math.log(class_total * ANGLES * SHIFTS)
    evidence = log_sum - log_orients
    weight = jnp.where(member, jnp.exp(jnp.where(member, picked - log_sum + log_orients, 0.0)), 0.0)
    numer_term, denom_term = align_terms(images, contrast, weight, rotation_id, shift_id)
    safe_class = jnp.where(member, local_class, 0)
    class_index = jnp.arange(group_classes, dtype=jnp.int32)
    slot = jnp.sum(
        jnp.where(safe_class[:, None] == class_index[None, :], owner[0][None, :], 0), axis=1
    )
    owning = (class_index[:, None] == jnp.where(member, slot, -1)[None, :]).astype(jnp.float32)
    partial_numer = jnp.dot(owning, numer_term, precision=lax.Precision.HIGHEST)
    partial_denom = jnp.dot(owning, denom_term, precision=lax.Precision.HIGHEST)
    numerator, denominator = (
        lax.psum_scatter(partial_numer, "blk", scatter_dimension=0, tiled=True),
        lax.psum_scatter(partial_denom, "blk", scatter_dimension=0, tiled=True),
    )
    new_refs = finish(numerator, denominator, prior)[None]
    return (evidence, new_refs)


def solution(mesh):
    in_specs = (
        P("blk", None),
        P("blk"),
        P("blk", None),
        P("blk"),
        P("blk"),
        P("grp", "blk", None),
        P("grp", None),
        P(),
        P(),
    )
    out_specs = (P("blk"), P("grp", "blk", None))
    return jax.shard_map(shards, mesh=mesh, in_specs=in_specs, out_specs=out_specs, check_vma=False)
```

profile of v0, /device:TPU:0, one launch (start us, length us, event | category | flops | bytes accessed | tf_op | source)
XLA Modules:
  0.0 1281.4 jit_solution(13221657645334171205)
XLA Ops:
  10.8 98.4 %all_gather.3 = f32[1,64,1536]{2,0,1:T(1,128)S(1)} all-gather(f32[1,2,1536]{2,0,1:T(1,128)S(1)} %copy.46), channel_id=1, replica_groups=mesh['blk'=32,'grp'=4] {'blk'}, dimensions={1}, use_global_device_ids=true | all-gather | bytes 405504 | tf_op jit(solution)/shard_map/all_gather | solution.py:130
  115.3 786.5 %while.18 = (s32[]{:T(128)}, f32[256]{0:T(256)S(1)}, f32[256]{0:T(256)}, f32[256]{0:T(256)}, f32[32,2,1536]{2,1,0:T(2,128)S(1)}, /*index=5*/bf16[256,1536]{1,0:T...) while((s32[]{:T(128)}, f32[256]{0:T(256)S(1)}, ...), condition=%wide.region_5.6_spmd.clone, body=%wide.region_0.5_spmd.clone.sunk | while | flops 496573632 | bytes 14409568 | solution.py:144
  125.2 8.9 convert_element_type.90
  149.1 8.9 convert_element_type.90
  173.7 8.9 convert_element_type.90
  198.3 8.9 convert_element_type.90
  222.9 8.9 convert_element_type.90
  247.5 8.9 convert_element_type.90
  272.1 8.9 convert_element_type.90
  296.7 8.9 convert_element_type.90
  321.3 8.9 convert_element_type.90
  345.9 8.9 convert_element_type.90
  370.5 8.9 convert_element_type.90
  395.1 8.9 convert_element_type.90
  419.7 8.9 convert_element_type.90
  444.3 8.9 convert_element_type.90
  468.9 8.9 convert_element_type.90
  493.5 8.9 convert_element_type.90
  518.1 8.9 convert_element_type.90
  542.7 8.9 convert_element_type.90
  567.3 8.9 convert_element_type.90
  887.1 8.9 convert_element_type.90
  942.7 176.4 %all-reduce.1 = f32[64,24]{1,0:T(8,128)S(1)} all-reduce(f32[64,24]{1,0:T(8,128)S(1)} %fusion.44), channel_id=3, replica_groups=mesh['blk'=32,'grp'=4] {'blk'}, use_global_device_ids=true, to_apply=%region_10.11.clone | all-reduce | flops 1536 | bytes 12288
  1119.3 153.9 %all-reduce.4.cloned.1.call-done = f32[64,1536]{1,0:T(8,128)} async-done(((f32[64,1536]{1,0:T(8,128)}), f32[64,1536]{1,0:T(8,128)}) %all-reduce.4.cloned.1.call-update) | async-done | bytes 393232
  (937 shorter events, 656.9 us)
Async XLA Ops:
  7.2 106.8 %copy-start.2 = (s32[256]{0:T(256)S(1)}, s32[256]{0:T(256)}, u32[]{:S(2)}) copy-start(s32[256]{0:T(256)} %param.14) | copy-start | bytes 3076
  7.2 107.5 %copy-start.3 = (s32[256,1]{0,1:T(1,128)S(1)}, s32[256,1]{0,1:T(1,128)}, u32[]{:S(2)}) copy-start(s32[256,1]{0,1:T(1,128)} %param.13) | copy-start | bytes 3076
  7.2 108.1 %copy-start.1 = (s32[256]{0:T(256)S(1)}, s32[256]{0:T(256)}, u32[]{:S(2)}) copy-start(s32[256]{0:T(256)} %param.15) | copy-start | bytes 3076
  7.2 1266.0 %all-reduce.4.cloned.1.call-start = ((), (), s32[]{:S(2)}) async-start(), calls=%async_computation | async-start | bytes 786432
  134.1 2.4 copy-start.6
  182.6 2.4 copy-start.6
  207.2 2.4 copy-start.6
  231.8 2.4 copy-start.6
  256.4 2.4 copy-start.6
  281.0 2.4 copy-start.6
  305.6 2.4 copy-start.6
  330.2 2.4 copy-start.6
  354.8 2.4 copy-start.6
  379.4 2.4 copy-start.6
  404.0 2.4 copy-start.6
  428.6 2.4 copy-start.6
  453.2 2.4 copy-start.6
  477.8 2.4 copy-start.6
  502.4 2.4 copy-start.6
  600.8 2.4 copy-start.6
  699.2 2.4 copy-start.6
  920.8 5.2 copy-start
  933.6 6.8 copy-start.5
  933.6 185.5 %copy-start.4 = (f32[24]{0:T(128)S(1)}, f32[24]{0:T(128)}, u32[]{:S(2)}) copy-start(f32[24]{0:T(128)} %param.19) | copy-start | bytes 292
  (15 other events, 36.1 us)
Sparse Core Ops, SparseCore 0:
  940.5 332.6 all-reduce.3
where the time goes:
time: 1290 us; the launch traced here: 1280 us
  other arithmetic  331 us (26%)
  local copies, waits for them, and re-layouts  329 us (26%)
  blocking collectives  287 us (22%)
  matrix products  163 us (13%)
  waiting for transfers between devices  154 us (12%)
  between operations  14.9 us (1%)
    convert_element_type x32, local copies, waits for them, and re-layouts, make_templates(): stacked.reshape(block_rows * ANGLES * SHIFTS, -1).astype(jnp.bfloat16)  285 us
    unnamed x1, blocking collectives  176 us
    unnamed x2, waiting for transfers between devices  154 us
    another operation x32, other arithmetic, make_templates(): stacked = jnp.stack([real_part, imag_part], axis=3)  139 us
    all_gather x1, blocking collectives, shards(): shard_piece = lax.all_gather(references, 'blk', axis=1, tiled=True)  98.4 us
    dot_general x32, matrix products, score_block(): lax.dot_general(templates, weighted, (((1,), (1,)), ((), ())), preferred_...  76.6 us
    another operation x32, other arithmetic  65.7 us
    dot_general x32, matrix products, score_block(): penalty = jnp.dot(power, contrast_power.T, precision=lax.Precision.HIGHEST)  50.4 us
  transfers between devices with their start and end apart: 1, of which 1 were waited for; matrix products, arithmetic and copies ran while one was open for 0% of the time, Pallas kernels for 0%

commit v1 on v0

v1 whole, which is shorter than its diff:
```python
import functools
import math

import jax
import jax.numpy as jnp
import numpy as np
from jax import lax
from jax.experimental import pallas as pl
from jax.experimental.pallas import tpu as pltpu
from jax.sharding import PartitionSpec as P

CYCLES = 24
ANGLES = 32
SHIFTS = 9
CL_DEV = 2
P_BLK = 256
FEAT = 1536
HALF = FEAT // 2
C_GRP = 64
GROUPS = 4
CLASSES = 256
BLKS = 32
ROWS = 2 * C_GRP
PAIRS = 8
KGRP = 6
WIDE = FEAT + 128
LOG_ORIENTS = math.log(CLASSES * ANGLES * SHIFTS)
HIGH = lax.Precision.HIGHEST
F32 = jnp.float32
BF16 = jnp.bfloat16


def slot_place(s):
    if s == 0:
        return PAIRS - 1, 0
    if s == 8:
        return PAIRS - 1, 1
    return (s - 1, 0) if s < 8 else (15 - s, 1)


def phase_np():
    radius = (np.arange(CYCLES) + 1.0) / (2.0 * CYCLES)
    bearing = 2.0 * np.pi / ANGLES * np.arange(ANGLES)
    index = np.arange(SHIFTS)
    dx, dy = index // 3 - 1.0, index % 3 - 1.0
    along = dx[:, None] * np.cos(bearing) + dy[:, None] * np.sin(bearing)
    return -2.0 * np.pi * radius[None, :, None] * along[:, None, :]


def dft_rows():
    theta = 2.0 * np.pi / ANGLES
    angle = np.arange(ANGLES)
    out = np.zeros((16, 2, ANGLES))
    for s in range(1, 16):
        out[s, 0] = np.cos(theta * s * angle)
        out[s, 1] = -np.sin(theta * s * angle)
    out[0, 0] = 1.0
    out[0, 1] = np.cos(np.pi * angle)
    return out


def dft_plain():
    base = dft_rows()
    out = np.zeros((16, 2, 2, 4, 2, 4, ANGLES))
    for q in range(2):
        for k in range(4):
            out[:, :, q, k, q, k, :] = base
    return out.reshape(256, 256)


def turn_table():
    phase = phase_np().reshape(SHIFTS, HALF)
    px, py = phase[7], phase[5]
    columns = [np.cos(px), np.sin(px), np.cos(py), np.sin(py)]
    return np.stack(columns + columns, axis=1).astype(np.float32)


def split(x):
    high = x.astype(np.float32).astype(jnp.bfloat16)
    low = (x - high.astype(np.float64)).astype(np.float32).astype(jnp.bfloat16)
    return high, low


def iota(shape, axis):
    return lax.broadcasted_iota(jnp.int32, shape, axis)


def as_column(row, n):
    same = iota((n, n), 0) == iota((n, n), 1)
    zero = jnp.zeros((), row.dtype)
    return jnp.sum(jnp.where(same, jnp.broadcast_to(row, (n, n)), zero), axis=1, keepdims=True)


def spread_cycles(row):
    column = as_column(row, CYCLES)
    hit = iota((CYCLES, HALF), 0) == iota((CYCLES, HALF), 1) // ANGLES
    return jnp.sum(jnp.where(hit, column, 0.0), axis=0, keepdims=True)


def rows_setup(group, defocus, cls, rot, shf, owner, crow_ref, key_ref, column_ref, turn_ref):
    local = cls - group * C_GRP
    member = (local >= 0) & (local < C_GRP)
    cls_col = as_column(cls, P_BLK)
    earlier = (cls_col == cls) & (iota((P_BLK, P_BLK), 0) < iota((P_BLK, P_BLK), 1))
    turn = jnp.sum(jnp.where(earlier, 1, 0), axis=0, keepdims=True)
    owner_col = as_column(owner, C_GRP)
    hit = iota((C_GRP, P_BLK), 0) == local
    slot = jnp.sum(jnp.where(hit, owner_col, 0), axis=0, keepdims=True)
    key = jnp.where(member, turn * C_GRP + slot, -1)
    key_ref[...] = key
    chosen = iota((ROWS, P_BLK), 0) == key
    pick = lambda row: jnp.sum(jnp.where(chosen, row, jnp.zeros((), row.dtype)), axis=1, keepdims=True)
    focus = jnp.broadcast_to(pick(defocus), (ROWS, 128))
    column_ref[...] = focus
    turn_ref[0] = jnp.broadcast_to(pick(rot), (ROWS, 128))
    turn_ref[1] = jnp.broadcast_to(pick(shf), (ROWS, 128))
    frequency = (iota((1, 128), 1).astype(F32) + 1.0) / CYCLES
    inside = iota((ROWS, 128), 1) < CYCLES
    crow_ref[...] = jnp.where(inside, -jnp.sin(focus * jnp.where(frequency <= 1.0, frequency * frequency, 0.0) + 0.15), 0.0)


def rows_part(g, first, second, table_cos, table_sin, y_ref, cexp_ref, key_ref, column_ref, turn_ref):
    chosen = (iota((ROWS, P_BLK), 0) == key_ref[...]).astype(BF16)
    real = jnp.dot(chosen, first, preferred_element_type=F32)
    imag = jnp.dot(chosen, second, preferred_element_type=F32)
    frequency = ((iota((1, 128), 1) // ANGLES + 4 * g).astype(F32) + 1.0) / CYCLES
    cexp = -jnp.sin(column_ref[...] * (frequency * frequency) + 0.15)
    cexp_ref[...] = cexp
    which = (iota((ROWS, 16), 1) == turn_ref[1][:, :16]).astype(F32)
    cos = jnp.dot(which, table_cos, precision=HIGH, preferred_element_type=F32)
    sin = jnp.dot(which, table_sin, precision=HIGH, preferred_element_type=F32)
    angle = iota((ROWS, 128), 1) % ANGLES
    parts = [cos * real + sin * imag, cos * imag - sin * real]
    for bit in range(5):
        step = 1 << bit
        on = (turn_ref[0] // step) % 2 == 1
        near = angle < ANGLES - step
        for q in range(2):
            x = parts[q]
            moved = jnp.where(near, pltpu.roll(x, 128 - step, 1), pltpu.roll(x, ANGLES - step, 1))
            parts[q] = jnp.where(on, moved, x)
    for q in range(2):
        y_ref[q] = parts[q] * cexp


def prep_kernel(
    group_ref,
    first_ref,
    second_ref,
    defocus_ref,
    cls_ref,
    rot_ref,
    shf_ref,
    owner_ref,
    inv_ref,
    cos_ref,
    sin_ref,
    turns_ref,
    plain_ref,
    what_ref,
    y_ref,
    crow_ref,
    cexp_ref,
    key_ref,
    cp_ref,
    column_ref,
    turn_ref,
    factor_ref,
):
    g = pl.program_id(0)

    @pl.when(g == 0)
    def _():
        defocus = defocus_ref[...]
        frequency = (iota((CYCLES, 1), 0).astype(F32) + 1.0) / CYCLES
        contrast = -jnp.sin((frequency * frequency) * defocus + 0.15)
        inv = as_column(inv_ref[...], CYCLES)
        factor = contrast * inv
        for j in range(KGRP):
            factor_ref[j, 0:4, :] = factor[4 * j : 4 * j + 4]
        cp_ref[...] = jnp.concatenate([contrast * factor, jnp.zeros((128 - CYCLES, P_BLK), F32)], axis=0)
        rows_setup(
            group_ref[0, 0],
            defocus,
            cls_ref[...],
            rot_ref[...],
            shf_ref[...],
            owner_ref[...],
            crow_ref,
            key_ref,
            column_ref,
            turn_ref,
        )

    wide = jnp.concatenate([jnp.broadcast_to(factor_ref[g, k : k + 1, :], (ANGLES, P_BLK)) for k in range(4)], axis=0)
    w0 = first_ref[...].astype(F32).T * wide
    w1 = second_ref[...].astype(F32).T * wide
    tables = [jnp.broadcast_to(turns_ref[:, j : j + 1], (128, P_BLK)) for j in range(4)]

    def moves(v0, v1, c, s):
        c0, c1, s0, s1 = c * v0, c * v1, s * v0, s * v1
        return [(c0 - s1, c1 + s0), (v0, v1), (c0 + s1, c1 - s0)]

    for i, (a0, a1) in enumerate(moves(w0, w1, tables[0], tables[1])):
        for j, (b0, b1) in enumerate(moves(a0, a1, tables[2], tables[3])):
            x = jnp.concatenate([b0, b1], axis=0).astype(BF16)
            res = jnp.dot(plain_ref[...], x, preferred_element_type=F32)
            res = (res[:256] + res[256:]).astype(BF16)
            for s in range(16):
                pair, side = slot_place(s)
                what_ref[3 * i + j, pair, 0, side] = res[16 * s : 16 * s + 16]
    rows_part(
        g, first_ref[...], second_ref[...], cos_ref[...], sin_ref[...], y_ref, cexp_ref, key_ref, column_ref, turn_ref
    )


def real_idft4(e0, e2, re, im):
    a, b = e0 + e2, e0 - e2
    return [a + re, b + im, a - re, b - im]


def real_idft8(c0, c4, c1, c2, c3):
    r = math.sqrt(0.5)
    even = real_idft4(c0 + c4, c2[0], c1[0] + c3[0], c1[1] - c3[1])
    hr, hi = c1[0] - c3[0], c1[1] + c3[1]
    odd = real_idft4(c0 - c4, c2[1], (hr + hi) * r, (hi - hr) * r)
    return even + odd


def real_idft16(a0, a8, a):
    plus = {m: (a[m][0] + a[8 - m][0], a[m][1] - a[8 - m][1]) for m in (1, 2, 3)}
    even = real_idft8(a0 + a8, a[4][0], plus[1], plus[2], plus[3])
    turned = {}
    for m in (1, 2, 3):
        hr, hi = a[m][0] - a[8 - m][0], a[m][1] + a[8 - m][1]
        if m == 2:
            r = math.sqrt(0.5)
            turned[m] = ((hr + hi) * r, (hi - hr) * r)
        else:
            c, s = math.cos(2.0 * math.pi * m / 16), math.sin(2.0 * math.pi * m / 16)
            turned[m] = (hr * c + hi * s, hi * c - hr * s)
    odd = real_idft8(a0 - a8, a[4][1], turned[1], turned[2], turned[3])
    return even + odd


def fold(values, op):
    while len(values) > 1:
        values = [op(values[i], values[i + 1]) if i + 1 < len(values) else values[i] for i in range(0, len(values), 2)]
    return values[0]


def factors(refs_ref, d_high, d_low, lhs_ref):
    scale = math.log2(math.e) / (ANGLES * math.sqrt(FEAT))
    pieces = []
    for h in range(3):
        halves = []
        for q in range(2):
            at = q * HALF + 256 * h
            both = jnp.concatenate([refs_ref[:, at : at + 128], refs_ref[:, at + 128 : at + 256]], axis=0)
            halves.append(both.T)
        pieces.append(jnp.concatenate(halves, axis=0))
    x = jnp.concatenate(pieces, axis=1)
    xh = x.astype(BF16)
    xl = (x - xh.astype(F32)).astype(BF16)
    res = jnp.dot(d_high, xh, preferred_element_type=F32)
    res = res + (jnp.dot(d_low, xh, preferred_element_type=F32) + jnp.dot(d_high, xl, preferred_element_type=F32))
    res = res * scale
    left = iota((8, 128), 1) < 64
    for pair in range(PAIRS):
        slots = (pair + 1, 15 - pair) if pair < PAIRS - 1 else (0, 8)
        blocks = [[[None] * 4 for _ in range(KGRP)] for _ in range(2)]
        for h in range(3):
            lanes = slice(128 * h, 128 * (h + 1))
            v = [(res[16 * s : 16 * s + 8, lanes], res[16 * s + 8 : 16 * s + 16, lanes]) for s in slots]
            outs = []
            if pair < PAIRS - 1:
                m = pair + 1
                c, s = 2.0 * math.cos(2.0 * math.pi * m / ANGLES), 2.0 * math.sin(2.0 * math.pi * m / ANGLES)
                (r0, i0), (r1, i1) = v
                outs.append(((2.0 * r0, 2.0 * i0), (2.0 * r1, 2.0 * i1)))
                outs.append(((2.0 * i0, -2.0 * r0), (-2.0 * i1, 2.0 * r1)))
                outs.append(((c * r0 + s * i0, c * i0 - s * r0), (s * i1 - c * r1, -c * i1 - s * r1)))
                outs.append(((c * i0 - s * r0, -c * r0 - s * i0), (c * i1 + s * r1, s * i1 - c * r1)))
            else:
                (r0, i0), (r1, i1) = v
                zero = jnp.zeros_like(r0)
                outs.append(((r0, i0), (zero, zero)))
                outs.append(((zero, zero), (2.0 * r1, 2.0 * i1)))
                outs.append(((r0, -i0), (zero, zero)))
                outs.append(((zero, zero), (2.0 * i1, -2.0 * r1)))
            for side in range(2):
                for part in range(2):
                    tiles = [o[side][part] for o in outs]
                    for two in range(2):
                        first, second = tiles[2 * two], tiles[2 * two + 1]
                        lower = jnp.where(left, first, pltpu.roll(second, 64, 1))
                        upper = jnp.where(left, pltpu.roll(first, 64, 1), second)
                        blocks[side][2 * h][2 * two + part] = lower
                        blocks[side][2 * h + 1][2 * two + part] = upper
        for two in range(2):
            tall = jnp.concatenate(
                [blocks[side][g][2 * two + part] for g in range(KGRP) for side in range(2) for part in range(2)], axis=0
            )
            lhs_ref[pair, 128 * two : 128 * (two + 1), :] = tall.T.astype(BF16)


def main_kernel(
    refs_ref, what_ref, plain_ref, cp_ref, inv_ref, y_ref, cexp_ref, owner_ref, lse_ref, picked_ref,
    lhs_ref, pen_ref, coef_ref, peak_ref, total_ref
):
    step = pl.program_id(0)
    root = 1.0 / math.sqrt(FEAT)

    @pl.when(step == 0)
    def _():
        factors(refs_ref, plain_ref[:256], plain_ref[256:], lhs_ref)
        refs = refs_ref[...]
        cycle = (iota((FEAT, 128), 0) // ANGLES) % CYCLES
        summing = (cycle == iota((FEAT, 128), 1)).astype(F32)
        power = jnp.dot(refs * refs, summing, precision=HIGH, preferred_element_type=F32)
        penalty = jnp.dot(power, cp_ref[...], precision=HIGH, preferred_element_type=F32)
        pen_ref[...] = penalty * (0.5 * root * math.log2(math.e))
        peak_ref[...] = jnp.full((8, P_BLK), -1e30, F32)
        total_ref[...] = jnp.zeros((8, P_BLK), F32)
        place = (jnp.broadcast_to(owner_ref[...], (C_GRP, C_GRP)) == iota((C_GRP, C_GRP), 0)).astype(F32)
        placed = jnp.dot(place, refs, precision=HIGH, preferred_element_type=F32)
        inv = spread_cycles(inv_ref[...])
        for o in range(2):
            rows = slice(C_GRP * o, C_GRP * (o + 1))
            cexp = cexp_ref[rows, :]
            amount = jnp.zeros((C_GRP, HALF), F32)
            for q in range(2):
                v = placed[:, HALF * q : HALF * (q + 1)]
                scaled = cexp * v
                amount = amount + (y_ref[q, rows, :] * v - 0.5 * scaled * scaled)
            picked_ref[rows, :] = jnp.broadcast_to(
                jnp.sum(amount * inv, axis=1, keepdims=True) * root, (C_GRP, 128)
            )

    for pair in range(PAIRS):
        coef_ref[pair] = jnp.dot(lhs_ref[pair], what_ref[0, pair].reshape(192, P_BLK), preferred_element_type=F32)
    for half in range(2):
        lanes = slice(128 * half, 128 * (half + 1))
        peak, total = peak_ref[:, lanes], total_ref[:, lanes]
        for cb in range(C_GRP // 8):
            take = lambda pair, o: coef_ref[pair, 64 * o + 8 * cb : 64 * o + 8 * cb + 8, lanes]
            pen = pen_ref[8 * cb : 8 * cb + 8, lanes]
            out = []
            for o in (0, 2):
                a = {m: (take(m - 1, o), take(m - 1, o + 1)) for m in range(1, 8)}
                out += real_idft16(take(7, o) - pen, take(7, o + 1), a)
            fresh = jnp.maximum(peak, fold(out, jnp.maximum))
            total = total * jnp.exp2(peak - fresh) + fold([jnp.exp2(x - fresh) for x in out], jnp.add)
            peak = fresh
        peak_ref[:, lanes] = peak
        total_ref[:, lanes] = total

    @pl.when(step == SHIFTS - 1)
    def _():
        peak, total = peak_ref[...], total_ref[...]
        top = jnp.max(peak, axis=0, keepdims=True)
        amount = jnp.sum(total * jnp.exp2(peak - top), axis=0, keepdims=True)
        lse = top * math.log(2.0) + jnp.log(amount)
        lse_ref[...] = jnp.concatenate([lse[:, :128], lse[:, 128:], jnp.zeros((6, 128), F32)], axis=0)


def weigh_kernel(lse_ref, picked_ref, key_ref, y_ref, crow_ref, out_ref):
    lse = jnp.concatenate([lse_ref[0:1, :], lse_ref[1:2, :]], axis=1)
    chosen = iota((ROWS, P_BLK), 0) == key_ref[...]
    mine = jnp.sum(jnp.where(chosen, lse, 0.0), axis=1, keepdims=True)
    valid = jnp.sum(jnp.where(chosen, 1.0, 0.0), axis=1, keepdims=True) > 0.5
    weight = jnp.where(valid, jnp.exp(jnp.where(valid, picked_ref[:, 0:1] - mine + LOG_ORIENTS, 0.0)), 0.0)
    w0, w1 = weight[:C_GRP], weight[C_GRP:]
    for q in range(2):
        out_ref[:, HALF * q : HALF * (q + 1)] = w0 * y_ref[q, :C_GRP] + w1 * y_ref[q, C_GRP:]
    c0, c1 = crow_ref[:C_GRP], crow_ref[C_GRP:]
    out_ref[:, FEAT:] = w0 * c0 * c0 + w1 * c1 * c1


def finish_kernel(got_ref, prior_ref, out_ref):
    total = fold([got_ref[8 * j : 8 * j + 8, :] for j in range(8)], jnp.add)
    total = total[0:4] + total[4:8]
    total = total[0:2] + total[2:4]
    denom = jnp.concatenate([total[:, FEAT:], jnp.ones((6, 128), F32)], axis=0)
    expand = (iota((128, HALF), 0) == iota((128, HALF), 1) // ANGLES).astype(F32)
    wide = jnp.dot(denom, expand, precision=HIGH, preferred_element_type=F32)[0:2]
    wide = wide + spread_cycles(prior_ref[...])
    out_ref[:, :HALF] = total[:, :HALF] / wide
    out_ref[:, HALF:] = total[:, HALF:FEAT] / wide


def params(mib):
    return pltpu.CompilerParams(vmem_limit_bytes=mib << 20)


def whole(shape):
    return pl.BlockSpec(shape, lambda *_: (0,) * len(shape))


def shape(dims, dtype=F32):
    return jax.ShapeDtypeStruct(dims, dtype)


def merge(a, b):
    top = jnp.maximum(a, b)
    return top + jnp.log(jnp.exp(a - top) + jnp.exp(b - top))


def in_hbm(x):
    return pltpu.with_memory_space_constraint(x, pltpu.HBM)


def shards(tables, images, defocus, class_id, rotation_id, shift_id, references, owner, inv_noise, prior):
    cos, sin, turns, plain = [in_hbm(jnp.asarray(v)) for v in tables]
    mine = references[0]
    refs = lax.all_to_all(
        jnp.broadcast_to(mine[None], (BLKS,) + mine.shape).reshape(-1, FEAT), "blk", 0, 0, tiled=True
    )
    group = lax.axis_index("grp").astype(jnp.int32).reshape(1, 1)
    row = lambda v: in_hbm(v.reshape(1, -1))
    inv = row(inv_noise)
    owner = in_hbm(owner)
    images = in_hbm(images)
    what, y, crow, cexp, key, cp = pl.pallas_call(
        prep_kernel,
        grid=(KGRP,),
        in_specs=[
            pl.BlockSpec(memory_space=pltpu.SMEM),
            pl.BlockSpec((P_BLK, 128), lambda g: (0, g)),
            pl.BlockSpec((P_BLK, 128), lambda g: (0, g + KGRP)),
        ]
        + [whole((1, P_BLK))] * 4
        + [whole((1, C_GRP)), whole((1, CYCLES))]
        + [pl.BlockSpec((16, 128), lambda g: (0, g))] * 2
        + [pl.BlockSpec((128, 8), lambda g: (g, 0)), whole((512, 256))],
        out_specs=[
            pl.BlockSpec((SHIFTS, PAIRS, 1, 2, 16, P_BLK), lambda g: (0, 0, g, 0, 0, 0)),
            pl.BlockSpec((2, ROWS, 128), lambda g: (0, 0, g)),
            whole((ROWS, 128)),
            pl.BlockSpec((ROWS, 128), lambda g: (0, g)),
            whole((1, P_BLK)),
            whole((128, P_BLK)),
        ],
        out_shape=[
            pltpu.HBM((SHIFTS, PAIRS, KGRP, 2, 16, P_BLK), BF16),
            shape((2, ROWS, HALF)),
            shape((ROWS, 128)),
            shape((ROWS, HALF)),
            shape((1, P_BLK), jnp.int32),
            shape((128, P_BLK)),
        ],
        scratch_shapes=[
            pltpu.VMEM((ROWS, 128), F32),
            pltpu.VMEM((2, ROWS, 128), jnp.int32),
            pltpu.VMEM((KGRP, 8, P_BLK), F32),
        ],
        compiler_params=params(40),
        cost_estimate=pl.CostEstimate(flops=4 << 30, bytes_accessed=24 << 20, transcendentals=0),
        name="prep",
    )(
        group,
        images,
        images,
        row(defocus),
        row(class_id),
        row(rotation_id),
        row(shift_id),
        owner,
        inv,
        cos,
        sin,
        turns,
        plain,
    )
    what = in_hbm(what)
    lse, picked = pl.pallas_call(
        main_kernel,
        grid=(SHIFTS,),
        in_specs=[
            whole((C_GRP, FEAT)),
            pl.BlockSpec((1, PAIRS, KGRP, 2, 16, P_BLK), lambda t: (t, 0, 0, 0, 0, 0)),
            whole((512, 256)),
            whole((128, P_BLK)),
            whole((1, CYCLES)),
            whole((2, ROWS, HALF)),
            whole((ROWS, HALF)),
            whole((1, C_GRP)),
        ],
        out_specs=[whole((8, 128)), whole((ROWS, 128))],
        out_shape=[shape((8, 128)), shape((ROWS, 128))],
        scratch_shapes=[
            pltpu.VMEM((PAIRS, 256, 192), BF16),
            pltpu.VMEM((C_GRP, P_BLK), F32),
            pltpu.VMEM((PAIRS, 256, P_BLK), F32),
            pltpu.VMEM((8, P_BLK), F32),
            pltpu.VMEM((8, P_BLK), F32),
        ],
        compiler_params=params(40),
        name="score",
    )(refs, what, plain, cp, inv, y, cexp, owner)
    lse = merge(lse, lax.ppermute(lse, "grp", [(0, 1), (1, 0), (2, 3), (3, 2)]))
    lse = merge(lse, lax.ppermute(lse, "grp", [(0, 2), (2, 0), (1, 3), (3, 1)]))
    evidence = lse[:2].reshape(P_BLK) - LOG_ORIENTS
    partial = pl.pallas_call(
        weigh_kernel, out_shape=shape((C_GRP, WIDE)), compiler_params=params(16), name="weigh"
    )(lse, picked, key, y, crow)
    got = lax.all_to_all(partial, "blk", 0, 0, tiled=True)
    new_refs = pl.pallas_call(
        finish_kernel, out_shape=shape((CL_DEV, FEAT)), compiler_params=params(16), name="finish"
    )(got, row(prior))
    return (evidence, new_refs[None])


def solution(mesh):
    in_specs = (
        P("blk", None),
        P("blk"),
        P("blk", None),
        P("blk"),
        P("blk"),
        P("grp", "blk", None),
        P("grp", None),
        P(),
        P(),
    )
    out_specs = (P("blk"), P("grp", "blk", None))
    phase = phase_np().reshape(SHIFTS, HALF)
    pad = np.zeros((16 - SHIFTS, HALF))
    cos = np.concatenate([np.cos(phase), pad]).astype(np.float32)
    sin = np.concatenate([np.sin(phase), pad]).astype(np.float32)
    tables = (cos, sin, turn_table(), np.concatenate(split(dft_plain())))
    return jax.shard_map(
        functools.partial(shards, tables), mesh=mesh, in_specs=in_specs, out_specs=out_specs, check_vma=False
    )
```

time: 1290 us -> 69.7 us (0.05)
  other arithmetic: 331 us -> 0.59 us
  local copies, waits for them, and re-layouts: 329 us -> 3.11 us
  blocking collectives: 287 us -> 0 us
  matrix products: 163 us -> 0 us
  waiting for transfers between devices: 154 us -> 14.9 us
  Pallas kernels: 0 us -> 28.4 us
  starting transfers between devices: 0.04 us -> 21.5 us
  between operations: 14.9 us -> 0.69 us
    convert_element_type x32 -> x0, local copies, waits for them, and re-layouts: 285 us -> none  [make_templates(): stacked.reshape(block_rows * ANGLES * SHIFTS, -1).astype(jnp.bfloat16)]
    another operation x65 -> x0, other arithmetic: 205 us -> none  [the longest x32 139 us: make_templates(): stacked = jnp.stack([real_part, imag_part], axis=3)]
    unnamed x1 -> x0, blocking collectives: 176 us -> none
    dot_general x101 -> x0, matrix products: 163 us -> none  [the longest x32 76.6 us: score_block(): lax.dot_general(templates, weighted, (((1,), (1,)), ((), ())), preferred_...]
    unnamed x2 -> x0, waiting for transfers between devices: 154 us -> none
    all_gather x1 -> x0, blocking collectives: 98.4 us -> none  [shards(): shard_piece = lax.all_gather(references, 'blk', axis=1, tiled=True)]
    add x66 -> x2, other arithmetic: 43.5 us -> 0.02 us  [merge(): return top + jnp.log(jnp.exp(a - top) + jnp.exp(b - top))]
    pallas_call x0 -> x4, Pallas kernels: none -> 28.4 us  [the longest x1 13.9 us: shards(): pl.pallas_call(prep_kernel, grid=(KGRP,), in_specs=[pl.BlockSpec(memory_s...]
  transfers between devices with their start and end apart: 1 -> 4, of which waited for: 1 -> 3; matrix products, arithmetic and copies ran while one was open for 0% -> 1% of each run, Pallas kernels for 0% -> 20%
where the time goes in v1:
time: 69.7 us; the launch traced here: 69.2 us
  Pallas kernels  28.4 us (41%)
  starting transfers between devices  21.5 us (31%)
  waiting for transfers between devices  14.9 us (21%)
  local copies, waits for them, and re-layouts  3.11 us (4%)
    pallas_call x1, Pallas kernels, shards(): pl.pallas_call(prep_kernel, grid=(KGRP,), in_specs=[pl.BlockSpec(memory_s...  13.9 us
    pallas_call x1, Pallas kernels, shards(): pl.pallas_call(main_kernel, grid=(SHIFTS,), in_specs=[whole((C_GRP, FEAT)...  12.8 us
    all_to_all x1, starting transfers between devices, shards(): lax.all_to_all(jnp.broadcast_to(mine[None], (BLKS,) + mine.shape).reshape...  10.9 us
    all_to_all x1, waiting for transfers between devices, shards(): got = lax.all_to_all(partial, 'blk', 0, 0, tiled=True)  10.7 us
    all_to_all x1, starting transfers between devices, shards(): got = lax.all_to_all(partial, 'blk', 0, 0, tiled=True)  9.83 us
    ppermute x1, waiting for transfers between devices, shards(): lse = merge(lse, lax.ppermute(lse, 'grp', [(0, 2), (2, 0), (1, 3), (3, 1)]))  3.02 us
    broadcast_in_dim x1, local copies, waits for them, and re-layouts, shards(): jnp.broadcast_to(mine[None], (BLKS,) + mine.shape).reshape(-1, FEAT)  1.56 us
    pallas_call x1, Pallas kernels, shards(): pl.pallas_call(finish_kernel, out_shape=shape((CL_DEV, FEAT)), compiler_p...  1.48 us
  transfers between devices with their start and end apart: 4, of which 3 were waited for; matrix products, arithmetic and copies ran while one was open for 1% of the time, Pallas kernels for 20%

profile of v1, /device:TPU:0, one launch (start us, length us, event | category | flops | bytes accessed | tf_op | source)
XLA Modules:
  0.0 69.2 jit_solution(8494091520963166425)
XLA Ops:
  0.6 1.6 %broadcast_in_dim.11 = f32[32,2,1536]{2,1,0:T(2,128)} broadcast(f32[2,1536]{1,0:T(2,128)} %bitcast.11), dimensions={1,2} | broadcast | bytes 405504 | tf_op jit(solution)/shard_map/broadcast_in_dim | solution.py:417
  2.2 10.9 %all-to-all-start = ((f32[32,2,1536]{2,1,0:T(2,128)}), f32[32,2,1536]{2,1,0:T(2,128)S(1)}, u32[]{:S(2)}, u32[]{:S(2)}) async-start(f32[32,2,1536]{2,1,0:T(2,128)} %broadcast_in_dim.11), calls=%async_computation | async-start | bytes 786432 | tf_op jit(solution)/shard_map/all_to_all | solution.py:416
  13.1 13.9 %prep.1 = (bf16[9,8,6,2,16,256]{5,4,3,2,1,0:T(8,128)(2,1)}, f32[2,128,768]{2,1,0:T(8,128)S(1)}, f32[128,128]{1,0:T(8,128)S(1)}, f32[128,768]{1,0:T(8,128)S(1)}, ...) custom-call(s32[1,1]{1,0:T(1,128)} %bitcast.1.group_ref, bf16[256,1536]{1,0:T(8,128)(2,1)} %second_ref.1, ...), custom_call_target="tpu_custom_call" | custom-call | flops 4294967296 | bytes 25165824 | tf_op jit(solution)/shard_map/prep/pallas_call | solution.py:424
  27.0 0.0 all-to-all-done
  27.0 0.3 all_to_all.13.refs_ref
  27.2 12.8 %score.1 = (f32[8,128]{1,0:T(8,128)S(1)}, f32[128,128]{1,0:T(8,128)S(1)}) custom-call(f32[64,1536]{1,0:T(8,128)S(1)} %all_to_all.13.refs_ref, bf16[9,8,6,2,16,256]{5,4,3,2,1,0:T(8,128)(2,1)} %get-tuple-element.10.what_ref, bf16[512,256]{1,0:T(8,128)(2,1)} %constant.18.clone.plain_ref, f32[128,256]{1,0:T(8,128)S(1)} %get-tuple-element.11.cp_ref, ...), custom_call_target="tpu_custom_call" | custom-call | tf_op jit(solution)/shard_map/score/pallas_call | solution.py:476
  40.0 0.1 collective-permute-start
  40.1 1.2 %collective-permute-done = f32[8,128]{1,0:T(8,128)S(1)} collective-permute-done((f32[8,128]{1,0:T(8,128)S(1)}, f32[8,128]{1,0:T(8,128)S(1)}, u32[]{:S(2)}, u32[]{:S(2)}) %collective-permute-start) | collective-permute-done | bytes 4128 | tf_op jit(solution)/shard_map/ppermute | solution.py:501
  41.3 0.7 collective-permute-start.1
  42.0 3.0 %collective-permute-done.1 = f32[8,128]{1,0:T(8,128)S(1)} collective-permute-done((f32[8,128]{1,0:T(8,128)S(1)}, f32[8,128]{1,0:T(8,128)S(1)}, u32[]{:S(2)}, u32[]{:S(2)}) %collective-permute-start.1) | collective-permute-done | bytes 4128 | tf_op jit(solution)/shard_map/ppermute | solution.py:502
  45.0 0.3 weigh.1
  45.3 1.0 %all_to_all.14 = f32[32,2,1664]{2,1,0:T(2,128)} reshape(f32[64,1664]{1,0:T(8,128)S(1)} %weigh.1) | data formatting | bytes 851968 | tf_op jit(solution)/shard_map/all_to_all | solution.py:507
  46.3 9.8 %all-to-all-start.1 = ((f32[32,2,1664]{2,1,0:T(2,128)}), f32[32,2,1664]{2,1,0:T(2,128)S(1)}, u32[]{:S(2)}, u32[]{:S(2)}) async-start(f32[32,2,1664]{2,1,0:T(2,128)} %all_to_all.14), calls=%async_computation.1 | async-start | bytes 851968 | tf_op jit(solution)/shard_map/all_to_all | solution.py:507
  56.1 0.6 add_bitcast_fusion
  56.7 10.7 %all-to-all-done.1 = f32[32,2,1664]{2,1,0:T(2,128)S(1)} async-done(((f32[32,2,1664]{2,1,0:T(2,128)}), f32[32,2,1664]{2,1,0:T(2,128)S(1)}, u32[]{:S(2)}, u32[]{:S(2)}) %all-to-all-start.1) | async-done | bytes 426016 | tf_op jit(solution)/shard_map/all_to_all | solution.py:507
  67.4 0.3 all_to_all.16.got_ref
  67.7 1.5 %finish.1 = f32[2,1536]{1,0:T(2,128)} custom-call(f32[64,1664]{1,0:T(8,128)S(1)} %all_to_all.16.got_ref, f32[1,24]{1,0:T(1,128)} %bitcast.15), custom_call_target="tpu_custom_call" | custom-call | tf_op jit(solution)/shard_map/finish/pallas_call | solution.py:508
  (2 shorter events, 0.0 us)
Async XLA Ops:
  2.2 24.8 %all-to-all-start = ((f32[32,2,1536]{2,1,0:T(2,128)}), f32[32,2,1536]{2,1,0:T(2,128)S(1)}, u32[]{:S(2)}, u32[]{:S(2)}) async-start(f32[32,2,1536]{2,1,0:T(2,128)} %broadcast_in_dim.11), calls=%async_computation | async-start | bytes 786432 | tf_op jit(solution)/shard_map/all_to_all | solution.py:416
  40.0 1.2 %collective-permute-start = (f32[8,128]{1,0:T(8,128)S(1)}, f32[8,128]{1,0:T(8,128)S(1)}, u32[]{:S(2)}, u32[]{:S(2)}) collective-permute-start(f32[8,128]{1,0:T(8,128)S(1)} %get-tuple-element.14), channel_id=1, source_target_pairs={{0,1},{1,0},{2,3},{3,2},{4,5},{5,4},{6,7},{7,6},{8,9},{9,8},{10,11... | collective-permute-start | bytes 12296 | tf_op jit(solution)/shard_map/ppermute | solution.py:501
  41.3 3.7 %collective-permute-start.1 = (f32[8,128]{1,0:T(8,128)S(1)}, f32[8,128]{1,0:T(8,128)S(1)}, u32[]{:S(2)}, u32[]{:S(2)}) collective-permute-start(f32[8,128]{1,0:T(8,128)S(1)} %log_add_fusion.1), channel_id=1, source_target_pairs={{0,2},{2,0},{1,3},{3,1},{4,6},{6,4},{5,7},{7,5},{8,10},{10,8},{9,1... | collective-permute-start | bytes 12296 | tf_op jit(solution)/shard_map/ppermute | solution.py:502
  46.3 21.1 %all-to-all-start.1 = ((f32[32,2,1664]{2,1,0:T(2,128)}), f32[32,2,1664]{2,1,0:T(2,128)S(1)}, u32[]{:S(2)}, u32[]{:S(2)}) async-start(f32[32,2,1664]{2,1,0:T(2,128)} %all_to_all.14), calls=%async_computation.1 | async-start | bytes 851968 | tf_op jit(solution)/shard_map/all_to_all | solution.py:507

commit v2 on v1

v2 whole, which is shorter than its diff:
```python
import functools
import math

import jax
import jax.numpy as jnp
import numpy as np
from jax import lax
from jax.experimental import pallas as pl
from jax.experimental.pallas import tpu as pltpu
from jax.sharding import PartitionSpec as P

CYCLES = 24
ANGLES = 32
SHIFTS = 9
CL_DEV = 2
P_BLK = 256
FEAT = 1536
HALF = FEAT // 2
C_GRP = 64
GROUPS = 4
CLASSES = 256
BLKS = 32
ROWS = 2 * C_GRP
PAIRS = 8
KGRP = 6
WIDE = FEAT + 128
LOG_ORIENTS = math.log(CLASSES * ANGLES * SHIFTS)
HIGH = lax.Precision.HIGHEST
F32 = jnp.float32
BF16 = jnp.bfloat16


def slot_place(s):
    if s == 0:
        return PAIRS - 1, 0
    if s == 8:
        return PAIRS - 1, 1
    return (s - 1, 0) if s < 8 else (15 - s, 1)


def phase_np():
    radius = (np.arange(CYCLES) + 1.0) / (2.0 * CYCLES)
    bearing = 2.0 * np.pi / ANGLES * np.arange(ANGLES)
    index = np.arange(SHIFTS)
    dx, dy = index // 3 - 1.0, index % 3 - 1.0
    along = dx[:, None] * np.cos(bearing) + dy[:, None] * np.sin(bearing)
    return -2.0 * np.pi * radius[None, :, None] * along[:, None, :]


def dft_rows():
    theta = 2.0 * np.pi / ANGLES
    angle = np.arange(ANGLES)
    out = np.zeros((16, 2, ANGLES))
    for s in range(1, 16):
        out[s, 0] = np.cos(theta * s * angle)
        out[s, 1] = -np.sin(theta * s * angle)
    out[0, 0] = 1.0
    out[0, 1] = np.cos(np.pi * angle)
    return out


def dft_plain():
    base = dft_rows()
    out = np.zeros((16, 2, 2, 4, 2, 4, ANGLES))
    for q in range(2):
        for k in range(4):
            out[:, :, q, k, q, k, :] = base
    return out.reshape(256, 256)


def turn_table():
    phase = phase_np().reshape(SHIFTS, HALF)
    px, py = phase[7], phase[5]
    columns = [np.cos(px), np.sin(px), np.cos(py), np.sin(py)]
    return np.stack(columns + columns, axis=1).astype(np.float32)


def phase_table():
    phase = phase_np().reshape(SHIFTS, HALF)
    rest = np.zeros((16, FEAT))
    rest[:SHIFTS] = np.concatenate([np.cos(phase), np.sin(phase)], axis=1)
    parts = []
    for _ in range(3):
        parts.append(rest.astype(np.float32).astype(jnp.bfloat16))
        rest = rest - parts[-1].astype(np.float64)
    return np.concatenate(parts)


def split(x):
    high = x.astype(np.float32).astype(jnp.bfloat16)
    low = (x - high.astype(np.float64)).astype(np.float32).astype(jnp.bfloat16)
    return high, low


def iota(shape, axis):
    return lax.broadcasted_iota(jnp.int32, shape, axis)


def as_column(row, n):
    same = iota((n, n), 0) == iota((n, n), 1)
    zero = jnp.zeros((), row.dtype)
    return jnp.sum(jnp.where(same, jnp.broadcast_to(row, (n, n)), zero), axis=1, keepdims=True)


def spread_cycles(row):
    column = as_column(row, CYCLES)
    hit = iota((CYCLES, HALF), 0) == iota((CYCLES, HALF), 1) // ANGLES
    return jnp.sum(jnp.where(hit, column, 0.0), axis=0, keepdims=True)


def parts_of(x):
    high = x.astype(BF16)
    rest = x - high.astype(F32)
    middle = rest.astype(BF16)
    return high, middle, (rest - middle.astype(F32)).astype(BF16)


def prep_kernel(group_ref, *refs):
    sources, refs = refs[:10], refs[10:]
    stored_ref, y_ref, crow_ref, cexp_ref, key_ref, cp_ref, where_ref, inv_ref, prior_ref, plain_ref, summing_ref = refs[:11]
    images_ref, defocus_ref, cls_ref, rot_ref, shf_ref, owner_ref, noise_ref, table_ref, turns_ref, sem = refs[11:21]
    raw_ref, what_ref, out_sem = refs[21:24]
    targets = (
        defocus_ref, cls_ref, rot_ref, shf_ref, owner_ref, noise_ref, raw_ref, images_ref, table_ref, turns_ref
    )
    copies = [pltpu.make_async_copy(sources[j], targets[j], sem.at[j]) for j in range(10)]
    copies.append(pltpu.make_async_copy(refs[24], plain_ref, sem.at[10]))
    copies.append(pltpu.make_async_copy(refs[25], summing_ref, sem.at[11]))
    for copy in copies:
        copy.start()
    for copy in copies[:7]:
        copy.wait()

    defocus, cls, owner = defocus_ref[...], cls_ref[...], owner_ref[...]
    frequency = (iota((CYCLES, 1), 0).astype(F32) + 1.0) / CYCLES
    contrast = -jnp.sin((frequency * frequency) * defocus + 0.15)
    noise = noise_ref[...]
    factor = contrast * as_column(noise, CYCLES)
    cp_ref[...] = contrast * factor
    inv_ref[...] = jnp.broadcast_to(spread_cycles(noise), (8, HALF))
    prior_ref[...] = jnp.zeros((8, 128), F32)
    prior_ref[:, :CYCLES] = jnp.broadcast_to(raw_ref[...], (8, CYCLES))

    local = cls - group_ref[0, 0] * C_GRP
    member = (local >= 0) & (local < C_GRP)
    cls_col = as_column(cls, P_BLK)
    earlier = (cls_col == cls) & (iota((P_BLK, P_BLK), 0) < iota((P_BLK, P_BLK), 1))
    turn = jnp.sum(jnp.where(earlier, 1, 0), axis=0, keepdims=True)
    owner_col = as_column(owner, C_GRP)
    hit = iota((C_GRP, P_BLK), 0) == local
    slot = jnp.sum(jnp.where(hit, owner_col, 0), axis=0, keepdims=True)
    key = jnp.where(member, turn * C_GRP + slot, -1)
    key_ref[...] = key
    where_ref[...] = (iota((C_GRP, C_GRP), 0) == owner).astype(F32)

    chosen = iota((ROWS, P_BLK), 0) == key
    pick = lambda row: jnp.sum(jnp.where(chosen, row, jnp.zeros((), row.dtype)), axis=1, keepdims=True)
    lane = iota((ROWS, 128), 1)
    freq = (lane[0:1].astype(F32) + 1.0) / CYCLES
    freq = jnp.where(freq <= 1.0, freq * freq, 0.0)
    crow = jnp.where(lane < CYCLES, -jnp.sin(pick(defocus) * freq + 0.15), 0.0)
    crow_ref[...] = crow
    expand = (iota((128, HALF), 0) == iota((128, HALF), 1) // ANGLES).astype(BF16)
    cexp = sum(jnp.dot(c, expand, preferred_element_type=F32) for c in parts_of(crow))
    cexp_ref[...] = cexp
    which = (iota((ROWS, 48), 1) % 16 == pick(shf_ref[...])).astype(BF16)
    source = (lane & ~(ANGLES - 1)) | ((lane + pick(rot_ref[...])) & (ANGLES - 1))
    for copy in copies[7:10]:
        copy.wait()
    phase = jnp.dot(which, table_ref[...], preferred_element_type=F32)
    gathered = jnp.dot(chosen.astype(BF16), images_ref[...], preferred_element_type=F32)
    for j in range(HALF // 128):
        lanes, others = slice(128 * j, 128 * (j + 1)), slice(HALF + 128 * j, HALF + 128 * (j + 1))
        cos, sin, real, imag = phase[:, lanes], phase[:, others], gathered[:, lanes], gathered[:, others]
        both = (cos * real + sin * imag, cos * imag - sin * real)
        for q in range(2):
            turned = jnp.take_along_axis(both[q], source, axis=1, mode="promise_in_bounds")
            y_ref[q, :, lanes] = turned * cexp[:, lanes]
    copies[10].wait()

    def moves(v0, v1, c, s):
        c0, c1, s0, s1 = c * v0, c * v1, s * v0, s * v1
        return [(c0 - s1, c1 + s0), (v0, v1), (c0 + s1, c1 - s0)]

    plain = plain_ref[:256]
    stores = []
    for g in range(KGRP):
        wide = jnp.concatenate(
            [jnp.broadcast_to(factor[4 * g + k : 4 * g + k + 1, :], (ANGLES, P_BLK)) for k in range(4)], axis=0
        )
        w0 = images_ref[:, 128 * g : 128 * (g + 1)].astype(F32).T * wide
        w1 = images_ref[:, HALF + 128 * g : HALF + 128 * (g + 1)].astype(F32).T * wide
        turns = turns_ref[128 * g : 128 * (g + 1), :]
        tables = [jnp.broadcast_to(turns[:, j : j + 1], (128, P_BLK)) for j in range(4)]
        for i, (a0, a1) in enumerate(moves(w0, w1, tables[0], tables[1])):
            for j, (b0, b1) in enumerate(moves(a0, a1, tables[2], tables[3])):
                x = jnp.concatenate([b0, b1], axis=0).astype(BF16)
                res = jnp.dot(plain, x, preferred_element_type=F32).astype(BF16)
                for s in range(16):
                    pair, side = slot_place(s)
                    what_ref[3 * i + j, pair, g, 16 * side : 16 * side + 16, :] = res[16 * s : 16 * s + 16]
            piece = slice(3 * i, 3 * i + 3)
            store = pltpu.make_async_copy(
                what_ref.at[piece, :, g], stored_ref.at[piece, :, g], out_sem.at[g, i]
            )
            store.start()
            stores.append(store)
    copies[11].wait()
    for store in stores:
        store.wait()


def real_idft4(e0, e2, re, im):
    a, b = e0 + e2, e0 - e2
    return [a + re, b + im, a - re, b - im]


def real_idft8(c0, c4, c1, c2, c3):
    r = math.sqrt(0.5)
    even = real_idft4(c0 + c4, c2[0], c1[0] + c3[0], c1[1] - c3[1])
    hr, hi = c1[0] - c3[0], c1[1] + c3[1]
    odd = real_idft4(c0 - c4, c2[1], (hr + hi) * r, (hi - hr) * r)
    return even + odd


def real_idft16(a0, a8, a):
    plus = {m: (a[m][0] + a[8 - m][0], a[m][1] - a[8 - m][1]) for m in (1, 2, 3)}
    even = real_idft8(a0 + a8, a[4][0], plus[1], plus[2], plus[3])
    turned = {}
    for m in (1, 2, 3):
        hr, hi = a[m][0] - a[8 - m][0], a[m][1] + a[8 - m][1]
        if m == 2:
            r = math.sqrt(0.5)
            turned[m] = ((hr + hi) * r, (hi - hr) * r)
        else:
            c, s = math.cos(2.0 * math.pi * m / 16), math.sin(2.0 * math.pi * m / 16)
            turned[m] = (hr * c + hi * s, hi * c - hr * s)
    odd = real_idft8(a0 - a8, a[4][1], turned[1], turned[2], turned[3])
    return even + odd


def fold(values, op):
    while len(values) > 1:
        values = [op(values[i], values[i + 1]) if i + 1 < len(values) else values[i] for i in range(0, len(values), 2)]
    return values[0]


def factors(refs, d_high, d_low, lhs_ref):
    scale = math.log2(math.e) / (ANGLES * math.sqrt(FEAT))
    pieces = []
    for h in range(3):
        halves = []
        for q in range(2):
            at = q * HALF + 256 * h
            both = jnp.concatenate([refs[:, at : at + 128], refs[:, at + 128 : at + 256]], axis=0)
            halves.append(both.T)
        pieces.append(jnp.concatenate(halves, axis=0))
    x = jnp.concatenate(pieces, axis=1)
    xh = x.astype(BF16)
    xl = (x - xh.astype(F32)).astype(BF16)
    res = jnp.dot(d_high, xh, preferred_element_type=F32)
    res = res + (jnp.dot(d_low, xh, preferred_element_type=F32) + jnp.dot(d_high, xl, preferred_element_type=F32))
    res = res * scale
    left = iota((8, 128), 1) < 64
    for pair in range(PAIRS):
        slots = (pair + 1, 15 - pair) if pair < PAIRS - 1 else (0, 8)
        blocks = [[[None] * 4 for _ in range(KGRP)] for _ in range(2)]
        for h in range(3):
            lanes = slice(128 * h, 128 * (h + 1))
            v = [(res[16 * s : 16 * s + 8, lanes], res[16 * s + 8 : 16 * s + 16, lanes]) for s in slots]
            outs = []
            if pair < PAIRS - 1:
                m = pair + 1
                c, s = 2.0 * math.cos(2.0 * math.pi * m / ANGLES), 2.0 * math.sin(2.0 * math.pi * m / ANGLES)
                (r0, i0), (r1, i1) = v
                outs.append(((2.0 * r0, 2.0 * i0), (2.0 * r1, 2.0 * i1)))
                outs.append(((2.0 * i0, -2.0 * r0), (-2.0 * i1, 2.0 * r1)))
                outs.append(((c * r0 + s * i0, c * i0 - s * r0), (s * i1 - c * r1, -c * i1 - s * r1)))
                outs.append(((c * i0 - s * r0, -c * r0 - s * i0), (c * i1 + s * r1, s * i1 - c * r1)))
            else:
                (r0, i0), (r1, i1) = v
                zero = jnp.zeros_like(r0)
                outs.append(((r0, i0), (zero, zero)))
                outs.append(((zero, zero), (2.0 * r1, 2.0 * i1)))
                outs.append(((r0, -i0), (zero, zero)))
                outs.append(((zero, zero), (2.0 * i1, -2.0 * r1)))
            for side in range(2):
                for part in range(2):
                    tiles = [o[side][part] for o in outs]
                    for two in range(2):
                        first, second = tiles[2 * two], tiles[2 * two + 1]
                        lower = jnp.where(left, first, pltpu.roll(second, 64, 1))
                        upper = jnp.where(left, pltpu.roll(first, 64, 1), second)
                        blocks[side][2 * h][2 * two + part] = lower
                        blocks[side][2 * h + 1][2 * two + part] = upper
        for two in range(2):
            tall = jnp.concatenate(
                [blocks[side][g][2 * two + part] for g in range(KGRP) for side in range(2) for part in range(2)], axis=0
            )
            lhs_ref[pair, 128 * two : 128 * (two + 1), :] = tall.T.astype(BF16)


def score_kernel(refs_ref, stored_ref, plain_ref, summing_ref, cp_ref, lse_ref, lhs_ref, pen_ref, even_ref, odd_ref, what_ref, sem):
    root = 1.0 / math.sqrt(FEAT)
    load = lambda t: pltpu.make_async_copy(stored_ref.at[t], what_ref.at[t], sem.at[t])
    for t in range(2):
        load(t).start()
    refs = refs_ref[...]
    factors(refs, plain_ref[:256], plain_ref[256:], lhs_ref)
    for t in range(2, SHIFTS):
        load(t).start()
    square = refs[:, :HALF] * refs[:, :HALF] + refs[:, HALF:] * refs[:, HALF:]
    power = jnp.dot(jnp.concatenate(parts_of(square), axis=0), summing_ref[...], preferred_element_type=F32)
    power = power[:C_GRP] + (power[C_GRP : 2 * C_GRP] + power[2 * C_GRP :])
    penalty = jnp.dot(power[:, :CYCLES], cp_ref[...], precision=HIGH, preferred_element_type=F32)
    pen_ref[...] = penalty * (0.5 * root * math.log2(math.e))

    def multiply(t, coef_ref):
        load(t).wait()
        for pair in range(PAIRS):
            right = what_ref[t, pair].reshape(192, P_BLK)
            coef_ref[pair] = jnp.dot(lhs_ref[pair], right, preferred_element_type=F32)

    def absorb(coef_ref, state):
        fresh_state = []
        for half in range(2):
            lanes = slice(128 * half, 128 * (half + 1))
            peak, total = state[half]
            for cb in range(C_GRP // 8):
                take = lambda pair, o: coef_ref[pair, 64 * o + 8 * cb : 64 * o + 8 * cb + 8, lanes]
                pen = pen_ref[8 * cb : 8 * cb + 8, lanes]
                out = []
                for o in (0, 2):
                    a = {m: (take(m - 1, o), take(m - 1, o + 1)) for m in range(1, 8)}
                    out += real_idft16(take(7, o) - pen, take(7, o + 1), a)
                fresh = jnp.maximum(peak, fold(out, jnp.maximum))
                total = total * jnp.exp2(peak - fresh) + fold([jnp.exp2(x - fresh) for x in out], jnp.add)
                peak = fresh
            fresh_state.append((peak, total))
        return fresh_state

    start = (jnp.full((8, 128), -1e30, F32), jnp.zeros((8, 128), F32))
    multiply(0, even_ref)

    def body(j, state):
        multiply(2 * j + 1, odd_ref)
        state = absorb(even_ref, state)
        multiply(2 * j + 2, even_ref)
        return absorb(odd_ref, state)

    state = lax.fori_loop(0, (SHIFTS - 1) // 2, body, [start, start])
    state = absorb(even_ref, state)
    rows = []
    for peak, total in state:
        top = jnp.max(peak, axis=0, keepdims=True)
        amount = jnp.sum(total * jnp.exp2(peak - top), axis=0, keepdims=True)
        rows.append(top * math.log(2.0) + jnp.log(amount))
    lse_ref[...] = jnp.concatenate(rows + [jnp.zeros((6, 128), F32)], axis=0)


def pick_kernel(refs_ref, y_ref, cexp_ref, where_ref, inv_ref, picked_ref):
    root = 1.0 / math.sqrt(FEAT)
    where = where_ref[...].astype(BF16)
    refs = refs_ref[...]
    placed = sum(jnp.dot(where, part, preferred_element_type=F32) for part in parts_of(refs))
    inv = inv_ref[0:1, :]
    for o in range(2):
        rows = slice(C_GRP * o, C_GRP * (o + 1))
        amount = jnp.zeros((C_GRP, HALF), F32)
        for q in range(2):
            v = placed[:, HALF * q : HALF * (q + 1)]
            scaled = cexp_ref[rows, :] * v
            amount = amount + (y_ref[q, rows, :] * v - 0.5 * scaled * scaled)
        picked_ref[rows, :] = jnp.broadcast_to(jnp.sum(amount * inv, axis=1, keepdims=True) * root, (C_GRP, 128))


def weigh_kernel(lse_ref, picked_ref, key_ref, y_ref, crow_ref, out_ref, evidence_ref):
    lse = jnp.concatenate([lse_ref[0:1, :], lse_ref[1:2, :]], axis=1)
    evidence_ref[...] = lse - LOG_ORIENTS
    chosen = iota((ROWS, P_BLK), 0) == key_ref[...]
    mine = jnp.sum(jnp.where(chosen, lse, 0.0), axis=1, keepdims=True)
    valid = jnp.sum(jnp.where(chosen, 1.0, 0.0), axis=1, keepdims=True) > 0.5
    weight = jnp.where(valid, jnp.exp(jnp.where(valid, picked_ref[:, 0:1] - mine + LOG_ORIENTS, 0.0)), 0.0)
    w0, w1 = weight[:C_GRP], weight[C_GRP:]

    def put(at, value):
        for j in range(BLKS):
            out_ref[j, :, at : at + 128] = value[2 * j : 2 * j + 2]

    for q in range(2):
        for j in range(HALF // 128):
            lanes = slice(128 * j, 128 * (j + 1))
            put(HALF * q + 128 * j, w0 * y_ref[q, :C_GRP, lanes] + w1 * y_ref[q, C_GRP:, lanes])
    c0, c1 = crow_ref[:C_GRP], crow_ref[C_GRP:]
    put(FEAT, w0 * c0 * c0 + w1 * c1 * c1)


def finish_kernel(got_ref, prior_ref, out_ref):
    total = fold([got_ref[j] for j in range(BLKS)], jnp.add)
    denom = jnp.concatenate([total[:, FEAT:] + prior_ref[0:2, :], jnp.ones((6, 128), F32)], axis=0)
    expand = (iota((128, HALF), 0) == iota((128, HALF), 1) // ANGLES).astype(BF16)
    wide = sum(jnp.dot(d, expand, preferred_element_type=F32) for d in parts_of(denom))[0:2]
    out_ref[:, :HALF] = total[:, :HALF] / wide
    out_ref[:, HALF:] = total[:, HALF:FEAT] / wide


def params(mib):
    return pltpu.CompilerParams(vmem_limit_bytes=mib << 20)


def whole(shape):
    return pl.BlockSpec(shape, lambda *_: (0,) * len(shape))


def shape(dims, dtype=F32):
    return jax.ShapeDtypeStruct(dims, dtype)


def merge(a, b):
    top = jnp.maximum(a, b)
    return top + jnp.log(jnp.exp(a - top) + jnp.exp(b - top))


def in_hbm(x):
    return pltpu.with_memory_space_constraint(x, pltpu.HBM)


def in_hbm(x):
    return pltpu.with_memory_space_constraint(x, pltpu.HBM)


def gather(mine):
    spread = jnp.broadcast_to(mine[None], (BLKS,) + mine.shape).reshape(-1, FEAT)
    return lax.all_to_all(spread, "blk", 0, 0, tiled=True)


def shards(tables, images, defocus, class_id, rotation_id, shift_id, references, owner, inv_noise, prior):
    table, turns, plain, summing = [in_hbm(jnp.asarray(v)) for v in tables]
    refs = gather(references[0])
    index = lambda name: lax.axis_index(name).astype(jnp.int32).reshape(1, 1)
    row = lambda v: in_hbm(v.reshape(1, -1))
    what, y, crow, cexp, key, cp, where, inv, prior, plain, summing = pl.pallas_call(
        lambda group, *refs: prep_kernel(group, *refs[:10], *refs[12:], *refs[10:12]),
        in_specs=[pl.BlockSpec(memory_space=pltpu.SMEM)] + [pl.BlockSpec(memory_space=pl.ANY)] * 12,
        out_specs=[pl.BlockSpec(memory_space=pltpu.HBM)] + [pl.BlockSpec(memory_space=pltpu.VMEM)] * 10,
        out_shape=[
            pltpu.HBM((SHIFTS, PAIRS, KGRP, 32, P_BLK), BF16),
            shape((2, ROWS, HALF)),
            shape((ROWS, 128)),
            shape((ROWS, HALF)),
            shape((1, P_BLK), jnp.int32),
            shape((CYCLES, P_BLK)),
            shape((C_GRP, C_GRP)),
            shape((8, HALF)),
            shape((8, 128)),
            shape((512, 256), BF16),
            shape((HALF, 128), BF16),
        ],
        scratch_shapes=[
            pltpu.VMEM((P_BLK, FEAT), BF16),
            pltpu.VMEM((1, P_BLK), F32),
            pltpu.VMEM((1, P_BLK), jnp.int32),
            pltpu.VMEM((1, P_BLK), jnp.int32),
            pltpu.VMEM((1, P_BLK), jnp.int32),
            pltpu.VMEM((1, C_GRP), jnp.int32),
            pltpu.VMEM((1, CYCLES), F32),
            pltpu.VMEM((48, FEAT), BF16),
            pltpu.VMEM((HALF, 8), F32),
            pltpu.SemaphoreType.DMA((12,)),
            pltpu.VMEM((1, CYCLES), F32),
            pltpu.VMEM((SHIFTS, PAIRS, KGRP, 32, P_BLK), BF16),
            pltpu.SemaphoreType.DMA((KGRP, 3)),
        ],
        compiler_params=params(24),
        cost_estimate=pl.CostEstimate(flops=4 << 30, bytes_accessed=9 << 20, transcendentals=0),
        name="prep",
    )(
        index("grp"),
        row(defocus),
        row(class_id),
        row(rotation_id),
        row(shift_id),
        in_hbm(owner),
        row(inv_noise),
        row(prior),
        in_hbm(images),
        table,
        turns,
        plain,
        summing,
    )
    lse = pl.pallas_call(
        score_kernel,
        in_specs=[
            pl.BlockSpec(memory_space=pltpu.VMEM),
            pl.BlockSpec(memory_space=pl.ANY),
            pl.BlockSpec(memory_space=pltpu.VMEM),
            pl.BlockSpec(memory_space=pltpu.VMEM),
            pl.BlockSpec(memory_space=pltpu.VMEM),
        ],
        out_shape=shape((8, 128)),
        scratch_shapes=[
            pltpu.VMEM((PAIRS, 256, 192), BF16),
            pltpu.VMEM((C_GRP, P_BLK), F32),
            pltpu.VMEM((PAIRS, 256, P_BLK), F32),
            pltpu.VMEM((PAIRS, 256, P_BLK), F32),
            pltpu.VMEM((SHIFTS, PAIRS, KGRP, 32, P_BLK), BF16),
            pltpu.SemaphoreType.DMA((SHIFTS,)),
        ],
        compiler_params=params(24),
        cost_estimate=pl.CostEstimate(flops=8 << 30, bytes_accessed=9 << 20, transcendentals=0),
        name="score",
    )(refs, in_hbm(what), plain, summing, cp)
    picked = pl.pallas_call(
        pick_kernel,
        out_shape=shape((ROWS, 128)),
        compiler_params=params(16),
        cost_estimate=pl.CostEstimate(flops=1 << 30, bytes_accessed=2 << 20, transcendentals=0),
        name="pick",
    )(refs, y, cexp, where, inv)
    lse = merge(lse, lax.ppermute(lse, "grp", [(0, 1), (1, 0), (2, 3), (3, 2)]))
    lse = merge(lse, lax.ppermute(lse, "grp", [(0, 2), (2, 0), (1, 3), (3, 1)]))
    partial, evidence = pl.pallas_call(
        weigh_kernel,
        out_shape=[shape((BLKS, CL_DEV, WIDE)), shape((1, P_BLK))],
        compiler_params=params(16),
        name="weigh",
    )(lse, picked, key, y, crow)
    got = lax.all_to_all(partial, "blk", 0, 0)
    new_refs = pl.pallas_call(
        finish_kernel, out_shape=shape((CL_DEV, FEAT)), compiler_params=params(16), name="finish"
    )(got, prior)
    return (evidence.reshape(P_BLK), new_refs[None])


def solution(mesh):
    in_specs = (
        P("blk", None),
        P("blk"),
        P("blk", None),
        P("blk"),
        P("blk"),
        P("grp", "blk", None),
        P("grp", None),
        P(),
        P(),
    )
    out_specs = (P("blk"), P("grp", "blk", None))
    summing = np.arange(HALF)[:, None] // ANGLES == np.arange(128)[None, :]
    tables = (phase_table(), turn_table(), np.concatenate(split(dft_plain())), summing.astype(jnp.bfloat16))
    return jax.shard_map(
        functools.partial(shards, tables), mesh=mesh, in_specs=in_specs, out_specs=out_specs, check_vma=False
    )
```

time: 69.7 us -> 56.2 us (0.81)
  blocking collectives: 0 us -> 15.6 us
  Pallas kernels: 28.4 us -> 17.2 us
  starting transfers between devices: 21.5 us -> 11.6 us
  waiting for transfers between devices: 14.9 us -> 8.93 us
  local copies, waits for them, and re-layouts: 3.11 us -> 1.82 us
    all_to_all x0 -> x1, blocking collectives: none -> 15.6 us  [shards(): got = lax.all_to_all(partial, 'blk', 0, 0)]
    pallas_call x3 -> x4, Pallas kernels: 26.9 us -> 16.4 us  [the longest x1 8.5 us: shards(): pl.pallas_call(score_kernel, in_specs=[pl.BlockSpec(memory_space=pltpu.VM...]
    all_to_all x2 -> x1, starting transfers between devices: 20.7 us -> 10.9 us  [gather(): return lax.all_to_all(spread, 'blk', 0, 0, tiled=True)]
    all_to_all x2 -> x1, waiting for transfers between devices: 10.7 us -> 5.3 us  [gather(): return lax.all_to_all(spread, 'blk', 0, 0, tiled=True)]
    all_to_all x3 -> x1, local copies, waits for them, and re-layouts: 1.55 us -> 0.27 us  [gather(): return lax.all_to_all(spread, 'blk', 0, 0, tiled=True)]
    pallas_call x1, Pallas kernels: 1.48 us -> 0.78 us  [shards(): pl.pallas_call(finish_kernel, out_shape=shape((CL_DEV, FEAT)), compiler_p...]
  transfers between devices with their start and end apart: 4 -> 3, of which waited for: 3 -> 3; matrix products, arithmetic and copies ran while one was open for 1% -> 0% of each run, Pallas kernels for 20% -> 13%
where the time goes in v2:
time: 56.2 us; the launch traced here: 55.9 us
  Pallas kernels  17.2 us (31%)
  blocking collectives  15.6 us (28%)
  starting transfers between devices  11.6 us (21%)
  waiting for transfers between devices  8.93 us (16%)
  local copies, waits for them, and re-layouts  1.82 us (3%)
  between operations  0.68 us (1%)
    all_to_all x1, blocking collectives, shards(): got = lax.all_to_all(partial, 'blk', 0, 0)  15.6 us
    all_to_all x1, starting transfers between devices, gather(): return lax.all_to_all(spread, 'blk', 0, 0, tiled=True)  10.9 us
    pallas_call x1, Pallas kernels, shards(): pl.pallas_call(score_kernel, in_specs=[pl.BlockSpec(memory_space=pltpu.VM...  8.5 us
    pallas_call x1, Pallas kernels, shards(): pl.pallas_call(lambda group, *refs: prep_kernel(group, *refs[:10], *refs[...  6.47 us
    all_to_all x1, waiting for transfers between devices, gather(): return lax.all_to_all(spread, 'blk', 0, 0, tiled=True)  5.3 us
    ppermute x1, waiting for transfers between devices, shards(): lse = merge(lse, lax.ppermute(lse, 'grp', [(0, 2), (2, 0), (1, 3), (3, 1)]))  2.48 us
    broadcast_in_dim x1, local copies, waits for them, and re-layouts, gather(): jnp.broadcast_to(mine[None], (BLKS,) + mine.shape).reshape(-1, FEAT)  1.55 us
    ppermute x1, waiting for transfers between devices, shards(): lse = merge(lse, lax.ppermute(lse, 'grp', [(0, 1), (1, 0), (2, 3), (3, 2)]))  1.15 us
  transfers between devices with their start and end apart: 3, of which 3 were waited for; matrix products, arithmetic and copies ran while one was open for 0% of the time, Pallas kernels for 13%

profile of v2, /device:TPU:0, one launch (start us, length us, event | category | flops | bytes accessed | tf_op | source)
XLA Modules:
  0.0 55.9 jit_solution(3531747493265659779)
XLA Ops:
  0.6 1.6 %broadcast_in_dim.11 = f32[32,2,1536]{2,1,0:T(2,128)} broadcast(f32[2,1536]{1,0:T(2,128)} %bitcast.11), dimensions={1,2} | broadcast | bytes 405504 | tf_op jit(solution)/shard_map/broadcast_in_dim | solution.py:433
  2.2 10.9 %all-to-all-start = ((f32[32,2,1536]{2,1,0:T(2,128)}), f32[32,2,1536]{2,1,0:T(2,128)S(1)}, u32[]{:S(2)}, u32[]{:S(2)}) async-start(f32[32,2,1536]{2,1,0:T(2,128)} %broadcast_in_dim.11), calls=%async_computation | async-start | bytes 786432 | tf_op jit(solution)/shard_map/all_to_all | solution.py:434
  13.1 6.5 %prep.1 = (bf16[9,8,6,32,256]{4,3,2,1,0:T(8,128)(2,1)}, f32[2,128,768]{2,1,0:T(8,128)S(1)}, f32[128,128]{1,0:T(8,128)S(1)}, f32[128,768]{1,0:T(8,128)S(1)}, s32[...) custom-call(s32[1,1]{1,0:T(1,128)} %bitcast.1.group, ...), custom_call_target="tpu_custom_call" | custom-call | flops 4294967296 | bytes 9437184 | tf_op jit(solution)/shard_map/prep/pallas_call | solution.py:442
  19.5 5.3 %all-to-all-done = f32[32,2,1536]{2,1,0:T(2,128)S(1)} async-done(((f32[32,2,1536]{2,1,0:T(2,128)}), f32[32,2,1536]{2,1,0:T(2,128)S(1)}, u32[]{:S(2)}, u32[]{:S(2)}) %all-to-all-start) | async-done | bytes 393248 | tf_op jit(solution)/shard_map/all_to_all | solution.py:434
  24.8 0.3 all_to_all.9.refs_ref
  25.1 8.5 %score.1 = f32[8,128]{1,0:T(8,128)S(1)} custom-call(f32[64,1536]{1,0:T(8,128)S(1)} %all_to_all.9.refs_ref, bf16[9,8,6,32,256]{4,3,2,1,0:T(8,128)(2,1)} %get-tuple-element.15.stored_ref, bf16[512,256]{1,0:T(8,128)(2,1)S(1)} %get-tuple-element.16.plain_ref, bf16[768,128]{1,0:T(8,128)(2,1)S(1)} %get-tuple-element.17.summing_ref, ...), custom_call_target="tpu_custom_call" | custom-call | flops 8589934592 | bytes 9437184 | tf_op jit(solution)/shard_map/score/pallas_call | solution.py:492
  33.6 0.1 collective-permute-start
  33.7 1.2 %collective-permute-done = f32[8,128]{1,0:T(8,128)S(1)} collective-permute-done((f32[8,128]{1,0:T(8,128)S(1)}, f32[8,128]{1,0:T(8,128)S(1)}, u32[]{:S(2)}, u32[]{:S(2)}) %collective-permute-start) | collective-permute-done | bytes 4128 | tf_op jit(solution)/shard_map/ppermute | solution.py:521
  34.9 0.7 %collective-permute-start.1 = (f32[8,128]{1,0:T(8,128)S(1)}, f32[8,128]{1,0:T(8,128)S(1)}, u32[]{:S(2)}, u32[]{:S(2)}) collective-permute-start(f32[8,128]{1,0:T(8,128)S(1)} %log_add_fusion.1), channel_id=1, source_target_pairs={{0,2},{2,0},{1,3},{3,1},{4,6},{6,4},{5,7},{7,5},{8,10},{10,8},{9,1... | collective-permute-start | bytes 12296 | tf_op jit(solution)/shard_map/ppermute | solution.py:522
  35.6 0.5 pick.1.picked_ref
  36.1 2.5 %collective-permute-done.1 = f32[8,128]{1,0:T(8,128)S(1)} collective-permute-done((f32[8,128]{1,0:T(8,128)S(1)}, f32[8,128]{1,0:T(8,128)S(1)}, u32[]{:S(2)}, u32[]{:S(2)}) %collective-permute-start.1) | collective-permute-done | bytes 4128 | tf_op jit(solution)/shard_map/ppermute | solution.py:522
  38.6 0.9 %weigh.1 = (f32[32,2,1664]{2,1,0:T(2,128)S(1)}, f32[1,256]{1,0:T(1,128)}) custom-call(f32[8,128]{1,0:T(8,128)S(1)} %log_add_fusion.lse_ref, f32[128,128]{1,0:T(8,128)S(1)} %pick.1.picked_ref, s32[1,256]{1,0:T(1,128)S(1)} %get-tuple-element.23.key_ref, f32[2,128,768]{2,1,0:T(8,128)S(1)} %get-tuple-element.19.y_ref, f32[128,128]{1,0:T(8,128)S(1)} %get-tuple-element.24.crow_ref), custom_call_target="tpu_custom_call" | custom-call | tf_op jit(solution)/shard_map/weigh/pallas_call | solution.py:523
  39.5 15.6 %all_to_all.13.got_ref = f32[32,2,1664]{2,1,0:T(2,128)S(1)} all-to-all(f32[32,2,1664]{2,1,0:T(2,128)S(1)} %get-tuple-element.26), channel_id=1, replica_groups=mesh['blk'=32,'grp'=4] {'blk'}, dimensions={0} | all-to-all | bytes 851968 | tf_op jit(solution)/shard_map/all_to_all | solution.py:529
  55.1 0.8 %finish.1 = f32[2,1536]{1,0:T(2,128)} custom-call(f32[32,2,1664]{2,1,0:T(2,128)S(1)} %all_to_all.13.got_ref, f32[8,128]{1,0:T(8,128)S(1)} %get-tuple-element.27.prior_ref), custom_call_target="tpu_custom_call" | custom-call | tf_op jit(solution)/shard_map/finish/pallas_call | solution.py:530
  (2 shorter events, 0.0 us)
Async XLA Ops:
  2.2 22.7 %all-to-all-start = ((f32[32,2,1536]{2,1,0:T(2,128)}), f32[32,2,1536]{2,1,0:T(2,128)S(1)}, u32[]{:S(2)}, u32[]{:S(2)}) async-start(f32[32,2,1536]{2,1,0:T(2,128)} %broadcast_in_dim.11), calls=%async_computation | async-start | bytes 786432 | tf_op jit(solution)/shard_map/all_to_all | solution.py:434
  33.6 1.2 %collective-permute-start = (f32[8,128]{1,0:T(8,128)S(1)}, f32[8,128]{1,0:T(8,128)S(1)}, u32[]{:S(2)}, u32[]{:S(2)}) collective-permute-start(f32[8,128]{1,0:T(8,128)S(1)} %score.1), channel_id=1, source_target_pairs={{0,1},{1,0},{2,3},{3,2},{4,5},{5,4},{6,7},{7,6},{8,9},{9,8},{10,11... | collective-permute-start | bytes 12296 | tf_op jit(solution)/shard_map/ppermute | solution.py:521
  34.9 3.7 %collective-permute-start.1 = (f32[8,128]{1,0:T(8,128)S(1)}, f32[8,128]{1,0:T(8,128)S(1)}, u32[]{:S(2)}, u32[]{:S(2)}) collective-permute-start(f32[8,128]{1,0:T(8,128)S(1)} %log_add_fusion.1), channel_id=1, source_target_pairs={{0,2},{2,0},{1,3},{3,1},{4,6},{6,4},{5,7},{7,5},{8,10},{10,8},{9,1... | collective-permute-start | bytes 12296 | tf_op jit(solution)/shard_map/ppermute | solution.py:522

commit v3 on v2

--- a/solution.py
+++ b/solution.py
@@ -141,42 +141,8 @@
     prior_ref[...] = jnp.zeros((8, 128), F32)
     prior_ref[:, :CYCLES] = jnp.broadcast_to(raw_ref[...], (8, CYCLES))
 
-    local = cls - group_ref[0, 0] * C_GRP
-    member = (local >= 0) & (local < C_GRP)
-    cls_col = as_column(cls, P_BLK)
-    earlier = (cls_col == cls) & (iota((P_BLK, P_BLK), 0) < iota((P_BLK, P_BLK), 1))
-    turn = jnp.sum(jnp.where(earlier, 1, 0), axis=0, keepdims=True)
-    owner_col = as_column(owner, C_GRP)
-    hit = iota((C_GRP, P_BLK), 0) == local
-    slot = jnp.sum(jnp.where(hit, owner_col, 0), axis=0, keepdims=True)
-    key = jnp.where(member, turn * C_GRP + slot, -1)
-    key_ref[...] = key
-    where_ref[...] = (iota((C_GRP, C_GRP), 0) == owner).astype(F32)
-
-    chosen = iota((ROWS, P_BLK), 0) == key
-    pick = lambda row: jnp.sum(jnp.where(chosen, row, jnp.zeros((), row.dtype)), axis=1, keepdims=True)
-    lane = iota((ROWS, 128), 1)
-    freq = (lane[0:1].astype(F32) + 1.0) / CYCLES
-    freq = jnp.where(freq <= 1.0, freq * freq, 0.0)
-    crow = jnp.where(lane < CYCLES, -jnp.sin(pick(defocus) * freq + 0.15), 0.0)
-    crow_ref[...] = crow
-    expand = (iota((128, HALF), 0) == iota((128, HALF), 1) // ANGLES).astype(BF16)
-    cexp = sum(jnp.dot(c, expand, preferred_element_type=F32) for c in parts_of(crow))
-    cexp_ref[...] = cexp
-    which = (iota((ROWS, 48), 1) % 16 == pick(shf_ref[...])).astype(BF16)
-    source = (lane & ~(ANGLES - 1)) | ((lane + pick(rot_ref[...])) & (ANGLES - 1))
-    for copy in copies[7:10]:
-        copy.wait()
-    phase = jnp.dot(which, table_ref[...], preferred_element_type=F32)
-    gathered = jnp.dot(chosen.astype(BF16), images_ref[...], preferred_element_type=F32)
-    for j in range(HALF // 128):
-        lanes, others = slice(128 * j, 128 * (j + 1)), slice(HALF + 128 * j, HALF + 128 * (j + 1))
-        cos, sin, real, imag = phase[:, lanes], phase[:, others], gathered[:, lanes], gathered[:, others]
-        both = (cos * real + sin * imag, cos * imag - sin * real)
-        for q in range(2):
-            turned = jnp.take_along_axis(both[q], source, axis=1, mode="promise_in_bounds")
-            y_ref[q, :, lanes] = turned * cexp[:, lanes]
-    copies[10].wait()
+    for j in (7, 9, 10):
+        copies[j].wait()
 
     def moves(v0, v1, c, s):
         c0, c1, s0, s1 = c * v0, c * v1, s * v0, s * v1
@@ -205,6 +171,40 @@
             )
             store.start()
             stores.append(store)
+    local = cls - group_ref[0, 0] * C_GRP
+    member = (local >= 0) & (local < C_GRP)
+    cls_col = as_column(cls, P_BLK)
+    earlier = (cls_col == cls) & (iota((P_BLK, P_BLK), 0) < iota((P_BLK, P_BLK), 1))
+    turn = jnp.sum(jnp.where(earlier, 1, 0), axis=0, keepdims=True)
+    owner_col = as_column(owner, C_GRP)
+    hit = iota((C_GRP, P_BLK), 0) == local
+    slot = jnp.sum(jnp.where(hit, owner_col, 0), axis=0, keepdims=True)
+    key = jnp.where(member, turn * C_GRP + slot, -1)
+    key_ref[...] = key
+    where_ref[...] = (iota((C_GRP, C_GRP), 0) == owner).astype(F32)
+
+    chosen = iota((ROWS, P_BLK), 0) == key
+    pick = lambda row: jnp.sum(jnp.where(chosen, row, jnp.zeros((), row.dtype)), axis=1, keepdims=True)
+    lane = iota((ROWS, 128), 1)
+    freq = (lane[0:1].astype(F32) + 1.0) / CYCLES
+    freq = jnp.where(freq <= 1.0, freq * freq, 0.0)
+    crow = jnp.where(lane < CYCLES, -jnp.sin(pick(defocus) * freq + 0.15), 0.0)
+    crow_ref[...] = crow
+    expand = (iota((128, HALF), 0) == iota((128, HALF), 1) // ANGLES).astype(BF16)
+    cexp = sum(jnp.dot(c, expand, preferred_element_type=F32) for c in parts_of(crow))
+    cexp_ref[...] = cexp
+    which = (iota((ROWS, 48), 1) % 16 == pick(shf_ref[...])).astype(BF16)
+    source = (lane & ~(ANGLES - 1)) | ((lane + pick(rot_ref[...])) & (ANGLES - 1))
+    copies[8].wait()
+    phase = jnp.dot(which, table_ref[...], preferred_element_type=F32)
+    gathered = jnp.dot(chosen.astype(BF16), images_ref[...], preferred_element_type=F32)
+    for j in range(HALF // 128):
+        lanes, others = slice(128 * j, 128 * (j + 1)), slice(HALF + 128 * j, HALF + 128 * (j + 1))
+        cos, sin, real, imag = phase[:, lanes], phase[:, others], gathered[:, lanes], gathered[:, others]
+        both = (cos * real + sin * imag, cos * imag - sin * real)
+        for q in range(2):
+            turned = jnp.take_along_axis(both[q], source, axis=1, mode="promise_in_bounds")
+            y_ref[q, :, lanes] = turned * cexp[:, lanes]
     copies[11].wait()
     for store in stores:
         store.wait()
@@ -374,9 +374,8 @@
         picked_ref[rows, :] = jnp.broadcast_to(jnp.sum(amount * inv, axis=1, keepdims=True) * root, (C_GRP, 128))
 
 
-def weigh_kernel(lse_ref, picked_ref, key_ref, y_ref, crow_ref, out_ref, evidence_ref):
+def weigh_kernel(lse_ref, picked_ref, key_ref, y_ref, crow_ref, out_ref):
     lse = jnp.concatenate([lse_ref[0:1, :], lse_ref[1:2, :]], axis=1)
-    evidence_ref[...] = lse - LOG_ORIENTS
     chosen = iota((ROWS, P_BLK), 0) == key_ref[...]
     mine = jnp.sum(jnp.where(chosen, lse, 0.0), axis=1, keepdims=True)
     valid = jnp.sum(jnp.where(chosen, 1.0, 0.0), axis=1, keepdims=True) > 0.5
@@ -395,7 +394,9 @@
     put(FEAT, w0 * c0 * c0 + w1 * c1 * c1)
 
 
-def finish_kernel(got_ref, prior_ref, out_ref):
+def finish_kernel(got_ref, prior_ref, lse_ref, out_ref, evidence_ref):
+    evidence_ref[:, :128] = lse_ref[0:1, :] - LOG_ORIENTS
+    evidence_ref[:, 128:] = lse_ref[1:2, :] - LOG_ORIENTS
     total = fold([got_ref[j] for j in range(BLKS)], jnp.add)
     denom = jnp.concatenate([total[:, FEAT:] + prior_ref[0:2, :], jnp.ones((6, 128), F32)], axis=0)
     expand = (iota((128, HALF), 0) == iota((128, HALF), 1) // ANGLES).astype(BF16)
@@ -520,16 +521,19 @@
     )(refs, y, cexp, where, inv)
     lse = merge(lse, lax.ppermute(lse, "grp", [(0, 1), (1, 0), (2, 3), (3, 2)]))
     lse = merge(lse, lax.ppermute(lse, "grp", [(0, 2), (2, 0), (1, 3), (3, 1)]))
-    partial, evidence = pl.pallas_call(
+    partial = pl.pallas_call(
         weigh_kernel,
-        out_shape=[shape((BLKS, CL_DEV, WIDE)), shape((1, P_BLK))],
+        out_shape=shape((BLKS, CL_DEV, WIDE)),
         compiler_params=params(16),
         name="weigh",
     )(lse, picked, key, y, crow)
     got = lax.all_to_all(partial, "blk", 0, 0)
-    new_refs = pl.pallas_call(
-        finish_kernel, out_shape=shape((CL_DEV, FEAT)), compiler_params=params(16), name="finish"
-    )(got, prior)
+    new_refs, evidence = pl.pallas_call(
+        finish_kernel,
+        out_shape=[shape((CL_DEV, FEAT)), shape((1, P_BLK))],
+        compiler_params=params(16),
+        name="finish",
+    )(got, prior, lse)
     return (evidence.reshape(P_BLK), new_refs[None])
 
 

time: 56.2 us -> 55.2 us (0.982)
  Pallas kernels: 17.2 us -> 16.1 us
    pallas_call x2, Pallas kernels: 1.7 us -> 1.14 us  [the longest x1 0.78 us: shards(): pl.pallas_call(finish_kernel, out_shape=[shape((CL_DEV, FEAT)), shape((1,...]
  transfers between devices with their start and end apart: 3 -> 3, of which waited for: 3 -> 3; matrix products, arithmetic and copies ran while one was open for 0% -> 0% of each run, Pallas kernels for 13% -> 12%
where the time goes in v3:
time: 55.2 us; the launch traced here: 54.8 us
  Pallas kernels  16.1 us (29%)
  blocking collectives  15.1 us (27%)
  starting transfers between devices  11.6 us (21%)
  waiting for transfers between devices  9.42 us (17%)
  local copies, waits for them, and re-layouts  1.82 us (3%)
  between operations  0.68 us (1%)
    all_to_all x1, blocking collectives, shards(): got = lax.all_to_all(partial, 'blk', 0, 0)  15.1 us
    all_to_all x1, starting transfers between devices, gather(): return lax.all_to_all(spread, 'blk', 0, 0, tiled=True)  10.9 us
    pallas_call x1, Pallas kernels, shards(): pl.pallas_call(score_kernel, in_specs=[pl.BlockSpec(memory_space=pltpu.VM...  8.5 us
    pallas_call x1, Pallas kernels, shards(): pl.pallas_call(lambda group, *refs: prep_kernel(group, *refs[:10], *refs[...  5.98 us
    all_to_all x1, waiting for transfers between devices, gather(): return lax.all_to_all(spread, 'blk', 0, 0, tiled=True)  5.78 us
    ppermute x1, waiting for transfers between devices, shards(): lse = merge(lse, lax.ppermute(lse, 'grp', [(0, 2), (2, 0), (1, 3), (3, 1)]))  2.48 us
    broadcast_in_dim x1, local copies, waits for them, and re-layouts, gather(): jnp.broadcast_to(mine[None], (BLKS,) + mine.shape).reshape(-1, FEAT)  1.55 us
    ppermute x1, waiting for transfers between devices, shards(): lse = merge(lse, lax.ppermute(lse, 'grp', [(0, 1), (1, 0), (2, 3), (3, 2)]))  1.15 us
  transfers between devices with their start and end apart: 3, of which 3 were waited for; matrix products, arithmetic and copies ran while one was open for 0% of the time, Pallas kernels for 12%

profile of v3, /device:TPU:0, one launch (start us, length us, event | category | flops | bytes accessed | tf_op | source)
XLA Modules:
  0.0 54.8 jit_solution(9676632089851732808)
XLA Ops:
  0.6 1.6 %broadcast_in_dim.11 = f32[32,2,1536]{2,1,0:T(2,128)} broadcast(f32[2,1536]{1,0:T(2,128)} %bitcast.10), dimensions={1,2} | broadcast | bytes 405504 | tf_op jit(solution)/shard_map/broadcast_in_dim | solution.py:434
  2.2 10.9 %all-to-all-start = ((f32[32,2,1536]{2,1,0:T(2,128)}), f32[32,2,1536]{2,1,0:T(2,128)S(1)}, u32[]{:S(2)}, u32[]{:S(2)}) async-start(f32[32,2,1536]{2,1,0:T(2,128)} %broadcast_in_dim.11), calls=%async_computation | async-start | bytes 786432 | tf_op jit(solution)/shard_map/all_to_all | solution.py:435
  13.1 6.0 %prep.1 = (bf16[9,8,6,32,256]{4,3,2,1,0:T(8,128)(2,1)}, f32[2,128,768]{2,1,0:T(8,128)S(1)}, f32[128,128]{1,0:T(8,128)S(1)}, f32[128,768]{1,0:T(8,128)S(1)}, s32[...) custom-call(s32[1,1]{1,0:T(1,128)} %bitcast.1.group, ...), custom_call_target="tpu_custom_call" | custom-call | flops 4294967296 | bytes 9437184 | tf_op jit(solution)/shard_map/prep/pallas_call | solution.py:443
  19.1 5.8 %all-to-all-done = f32[32,2,1536]{2,1,0:T(2,128)S(1)} async-done(((f32[32,2,1536]{2,1,0:T(2,128)}), f32[32,2,1536]{2,1,0:T(2,128)S(1)}, u32[]{:S(2)}, u32[]{:S(2)}) %all-to-all-start) | async-done | bytes 393248 | tf_op jit(solution)/shard_map/all_to_all | solution.py:435
  24.8 0.3 all_to_all.9.refs_ref
  25.1 8.5 %score.1 = f32[8,128]{1,0:T(8,128)S(1)} custom-call(f32[64,1536]{1,0:T(8,128)S(1)} %all_to_all.9.refs_ref, bf16[9,8,6,32,256]{4,3,2,1,0:T(8,128)(2,1)} %get-tuple-element.15.stored_ref, bf16[512,256]{1,0:T(8,128)(2,1)S(1)} %get-tuple-element.16.plain_ref, bf16[768,128]{1,0:T(8,128)(2,1)S(1)} %get-tuple-element.17.summing_ref, ...), custom_call_target="tpu_custom_call" | custom-call | flops 8589934592 | bytes 9437184 | tf_op jit(solution)/shard_map/score/pallas_call | solution.py:493
  33.6 0.1 collective-permute-start
  33.7 1.2 %collective-permute-done = f32[8,128]{1,0:T(8,128)S(1)} collective-permute-done((f32[8,128]{1,0:T(8,128)S(1)}, f32[8,128]{1,0:T(8,128)S(1)}, u32[]{:S(2)}, u32[]{:S(2)}) %collective-permute-start) | collective-permute-done | bytes 4128 | tf_op jit(solution)/shard_map/ppermute | solution.py:522
  34.9 0.7 %collective-permute-start.1 = (f32[8,128]{1,0:T(8,128)S(1)}, f32[8,128]{1,0:T(8,128)S(1)}, u32[]{:S(2)}, u32[]{:S(2)}) collective-permute-start(f32[8,128]{1,0:T(8,128)S(1)} %log_add_fusion.1), channel_id=1, source_target_pairs={{0,2},{2,0},{1,3},{3,1},{4,6},{6,4},{5,7},{7,5},{8,10},{10,8},{9,1... | collective-permute-start | bytes 12296 | tf_op jit(solution)/shard_map/ppermute | solution.py:523
  35.6 0.5 pick.1.picked_ref
  36.1 2.5 %collective-permute-done.1 = f32[8,128]{1,0:T(8,128)S(1)} collective-permute-done((f32[8,128]{1,0:T(8,128)S(1)}, f32[8,128]{1,0:T(8,128)S(1)}, u32[]{:S(2)}, u32[]{:S(2)}) %collective-permute-start.1) | collective-permute-done | bytes 4128 | tf_op jit(solution)/shard_map/ppermute | solution.py:523
  38.6 0.4 weigh.1
  38.9 15.1 %all_to_all.13.got_ref = f32[32,2,1664]{2,1,0:T(2,128)S(1)} all-to-all(f32[32,2,1664]{2,1,0:T(2,128)S(1)} %weigh.1), channel_id=1, replica_groups=mesh['blk'=32,'grp'=4] {'blk'}, dimensions={0} | all-to-all | bytes 851968 | tf_op jit(solution)/shard_map/all_to_all | solution.py:530
  54.1 0.8 %finish.1 = (f32[2,1536]{1,0:T(2,128)}, f32[1,256]{1,0:T(1,128)}) custom-call(f32[32,2,1664]{2,1,0:T(2,128)S(1)} %all_to_all.13.got_ref, f32[8,128]{1,0:T(8,128)S(1)} %get-tuple-element.25.prior_ref, f32[8,128]{1,0:T(8,128)S(1)} %log_add_fusion.lse_ref), custom_call_target="tpu_custom_call" | custom-call | tf_op jit(solution)/shard_map/finish/pallas_call | solution.py:531
  (2 shorter events, 0.0 us)
Async XLA Ops:
  2.2 22.7 %all-to-all-start = ((f32[32,2,1536]{2,1,0:T(2,128)}), f32[32,2,1536]{2,1,0:T(2,128)S(1)}, u32[]{:S(2)}, u32[]{:S(2)}) async-start(f32[32,2,1536]{2,1,0:T(2,128)} %broadcast_in_dim.11), calls=%async_computation | async-start | bytes 786432 | tf_op jit(solution)/shard_map/all_to_all | solution.py:435
  33.6 1.2 %collective-permute-start = (f32[8,128]{1,0:T(8,128)S(1)}, f32[8,128]{1,0:T(8,128)S(1)}, u32[]{:S(2)}, u32[]{:S(2)}) collective-permute-start(f32[8,128]{1,0:T(8,128)S(1)} %score.1), channel_id=1, source_target_pairs={{0,1},{1,0},{2,3},{3,2},{4,5},{5,4},{6,7},{7,6},{8,9},{9,8},{10,11... | collective-permute-start | bytes 12296 | tf_op jit(solution)/shard_map/ppermute | solution.py:522
  34.9 3.7 %collective-permute-start.1 = (f32[8,128]{1,0:T(8,128)S(1)}, f32[8,128]{1,0:T(8,128)S(1)}, u32[]{:S(2)}, u32[]{:S(2)}) collective-permute-start(f32[8,128]{1,0:T(8,128)S(1)} %log_add_fusion.1), channel_id=1, source_target_pairs={{0,2},{2,0},{1,3},{3,1},{4,6},{6,4},{5,7},{7,5},{8,10},{10,8},{9,1... | collective-permute-start | bytes 12296 | tf_op jit(solution)/shard_map/ppermute | solution.py:523

commit v4 on v3

--- a/solution.py
+++ b/solution.py
@@ -215,9 +215,12 @@
     return [a + re, b + im, a - re, b - im]
 
 
-def real_idft8(c0, c4, c1, c2, c3):
-    r = math.sqrt(0.5)
-    even = real_idft4(c0 + c4, c2[0], c1[0] + c3[0], c1[1] - c3[1])
+def real_idft8(c0, c4, c1, c2, c3, scale=1.0):
+    r = scale * math.sqrt(0.5)
+    re, im = c1[0] + c3[0], c1[1] - c3[1]
+    if scale != 1.0:
+        re, im = re * scale, im * scale
+    even = real_idft4(c0 + c4, c2[0], re, im)
     hr, hi = c1[0] - c3[0], c1[1] + c3[1]
     odd = real_idft4(c0 - c4, c2[1], (hr + hi) * r, (hi - hr) * r)
     return even + odd
@@ -233,9 +236,9 @@
             r = math.sqrt(0.5)
             turned[m] = ((hr + hi) * r, (hi - hr) * r)
         else:
-            c, s = math.cos(2.0 * math.pi * m / 16), math.sin(2.0 * math.pi * m / 16)
-            turned[m] = (hr * c + hi * s, hi * c - hr * s)
-    odd = real_idft8(a0 - a8, a[4][1], turned[1], turned[2], turned[3])
+            t = math.tan(math.pi / 8)
+            turned[m] = (hr + hi * t, hi - hr * t) if m == 1 else (hr * t + hi, hi * t - hr)
+    odd = real_idft8(a0 - a8, a[4][1], turned[1], turned[2], turned[3], math.cos(math.pi / 8))
     return even + odd
 
 

time: 55.2 us -> 55.2 us (level)
  no operation moved by 1% of the time
where the time goes in v4:
time: 55.2 us; the launch traced here: 54.9 us
  Pallas kernels  16.2 us (29%)
  blocking collectives  15.1 us (27%)
  starting transfers between devices  11.6 us (21%)
  waiting for transfers between devices  9.42 us (17%)
  local copies, waits for them, and re-layouts  1.82 us (3%)
  between operations  0.68 us (1%)
    all_to_all x1, blocking collectives, shards(): got = lax.all_to_all(partial, 'blk', 0, 0)  15.1 us
    all_to_all x1, starting transfers between devices, gather(): return lax.all_to_all(spread, 'blk', 0, 0, tiled=True)  10.9 us
    pallas_call x1, Pallas kernels, shards(): pl.pallas_call(score_kernel, in_specs=[pl.BlockSpec(memory_space=pltpu.VM...  8.51 us
    pallas_call x1, Pallas kernels, shards(): pl.pallas_call(lambda group, *refs: prep_kernel(group, *refs[:10], *refs[...  5.98 us
    all_to_all x1, waiting for transfers between devices, gather(): return lax.all_to_all(spread, 'blk', 0, 0, tiled=True)  5.78 us
    ppermute x1, waiting for transfers between devices, shards(): lse = merge(lse, lax.ppermute(lse, 'grp', [(0, 2), (2, 0), (1, 3), (3, 1)]))  2.48 us
    broadcast_in_dim x1, local copies, waits for them, and re-layouts, gather(): jnp.broadcast_to(mine[None], (BLKS,) + mine.shape).reshape(-1, FEAT)  1.55 us
    ppermute x1, waiting for transfers between devices, shards(): lse = merge(lse, lax.ppermute(lse, 'grp', [(0, 1), (1, 0), (2, 3), (3, 2)]))  1.15 us
  transfers between devices with their start and end apart: 3, of which 3 were waited for; matrix products, arithmetic and copies ran while one was open for 0% of the time, Pallas kernels for 12%

profile of v4, /device:TPU:0, one launch (start us, length us, event | category | flops | bytes accessed | tf_op | source)
XLA Modules:
  0.0 54.9 jit_solution(4494929996777516948)
XLA Ops:
  0.6 1.6 %broadcast_in_dim.11 = f32[32,2,1536]{2,1,0:T(2,128)} broadcast(f32[2,1536]{1,0:T(2,128)} %bitcast.10), dimensions={1,2} | broadcast | bytes 405504 | tf_op jit(solution)/shard_map/broadcast_in_dim | solution.py:437
  2.2 10.9 %all-to-all-start = ((f32[32,2,1536]{2,1,0:T(2,128)}), f32[32,2,1536]{2,1,0:T(2,128)S(1)}, u32[]{:S(2)}, u32[]{:S(2)}) async-start(f32[32,2,1536]{2,1,0:T(2,128)} %broadcast_in_dim.11), calls=%async_computation | async-start | bytes 786432 | tf_op jit(solution)/shard_map/all_to_all | solution.py:438
  13.1 6.0 %prep.1 = (bf16[9,8,6,32,256]{4,3,2,1,0:T(8,128)(2,1)}, f32[2,128,768]{2,1,0:T(8,128)S(1)}, f32[128,128]{1,0:T(8,128)S(1)}, f32[128,768]{1,0:T(8,128)S(1)}, s32[...) custom-call(s32[1,1]{1,0:T(1,128)} %bitcast.1.group, ...), custom_call_target="tpu_custom_call" | custom-call | flops 4294967296 | bytes 9437184 | tf_op jit(solution)/shard_map/prep/pallas_call | solution.py:446
  19.1 5.8 %all-to-all-done = f32[32,2,1536]{2,1,0:T(2,128)S(1)} async-done(((f32[32,2,1536]{2,1,0:T(2,128)}), f32[32,2,1536]{2,1,0:T(2,128)S(1)}, u32[]{:S(2)}, u32[]{:S(2)}) %all-to-all-start) | async-done | bytes 393248 | tf_op jit(solution)/shard_map/all_to_all | solution.py:438
  24.8 0.3 all_to_all.9.refs_ref
  25.1 8.5 %score.1 = f32[8,128]{1,0:T(8,128)S(1)} custom-call(f32[64,1536]{1,0:T(8,128)S(1)} %all_to_all.9.refs_ref, bf16[9,8,6,32,256]{4,3,2,1,0:T(8,128)(2,1)} %get-tuple-element.15.stored_ref, bf16[512,256]{1,0:T(8,128)(2,1)S(1)} %get-tuple-element.16.plain_ref, bf16[768,128]{1,0:T(8,128)(2,1)S(1)} %get-tuple-element.17.summing_ref, ...), custom_call_target="tpu_custom_call" | custom-call | flops 8589934592 | bytes 9437184 | tf_op jit(solution)/shard_map/score/pallas_call | solution.py:496
  33.6 0.1 collective-permute-start
  33.7 1.2 %collective-permute-done = f32[8,128]{1,0:T(8,128)S(1)} collective-permute-done((f32[8,128]{1,0:T(8,128)S(1)}, f32[8,128]{1,0:T(8,128)S(1)}, u32[]{:S(2)}, u32[]{:S(2)}) %collective-permute-start) | collective-permute-done | bytes 4128 | tf_op jit(solution)/shard_map/ppermute | solution.py:525
  34.9 0.7 %collective-permute-start.1 = (f32[8,128]{1,0:T(8,128)S(1)}, f32[8,128]{1,0:T(8,128)S(1)}, u32[]{:S(2)}, u32[]{:S(2)}) collective-permute-start(f32[8,128]{1,0:T(8,128)S(1)} %log_add_fusion.1), channel_id=1, source_target_pairs={{0,2},{2,0},{1,3},{3,1},{4,6},{6,4},{5,7},{7,5},{8,10},{10,8},{9,1... | collective-permute-start | bytes 12296 | tf_op jit(solution)/shard_map/ppermute | solution.py:526
  35.6 0.5 pick.1.picked_ref
  36.1 2.5 %collective-permute-done.1 = f32[8,128]{1,0:T(8,128)S(1)} collective-permute-done((f32[8,128]{1,0:T(8,128)S(1)}, f32[8,128]{1,0:T(8,128)S(1)}, u32[]{:S(2)}, u32[]{:S(2)}) %collective-permute-start.1) | collective-permute-done | bytes 4128 | tf_op jit(solution)/shard_map/ppermute | solution.py:526
  38.6 0.4 weigh.1
  39.0 15.1 %all_to_all.13.got_ref = f32[32,2,1664]{2,1,0:T(2,128)S(1)} all-to-all(f32[32,2,1664]{2,1,0:T(2,128)S(1)} %weigh.1), channel_id=1, replica_groups=mesh['blk'=32,'grp'=4] {'blk'}, dimensions={0} | all-to-all | bytes 851968 | tf_op jit(solution)/shard_map/all_to_all | solution.py:533
  54.1 0.8 %finish.1 = (f32[2,1536]{1,0:T(2,128)}, f32[1,256]{1,0:T(1,128)}) custom-call(f32[32,2,1664]{2,1,0:T(2,128)S(1)} %all_to_all.13.got_ref, f32[8,128]{1,0:T(8,128)S(1)} %get-tuple-element.25.prior_ref, f32[8,128]{1,0:T(8,128)S(1)} %log_add_fusion.lse_ref), custom_call_target="tpu_custom_call" | custom-call | tf_op jit(solution)/shard_map/finish/pallas_call | solution.py:534
  (2 shorter events, 0.0 us)
Async XLA Ops:
  2.2 22.7 %all-to-all-start = ((f32[32,2,1536]{2,1,0:T(2,128)}), f32[32,2,1536]{2,1,0:T(2,128)S(1)}, u32[]{:S(2)}, u32[]{:S(2)}) async-start(f32[32,2,1536]{2,1,0:T(2,128)} %broadcast_in_dim.11), calls=%async_computation | async-start | bytes 786432 | tf_op jit(solution)/shard_map/all_to_all | solution.py:438
  33.6 1.2 %collective-permute-start = (f32[8,128]{1,0:T(8,128)S(1)}, f32[8,128]{1,0:T(8,128)S(1)}, u32[]{:S(2)}, u32[]{:S(2)}) collective-permute-start(f32[8,128]{1,0:T(8,128)S(1)} %score.1), channel_id=1, source_target_pairs={{0,1},{1,0},{2,3},{3,2},{4,5},{5,4},{6,7},{7,6},{8,9},{9,8},{10,11... | collective-permute-start | bytes 12296 | tf_op jit(solution)/shard_map/ppermute | solution.py:525
  34.9 3.7 %collective-permute-start.1 = (f32[8,128]{1,0:T(8,128)S(1)}, f32[8,128]{1,0:T(8,128)S(1)}, u32[]{:S(2)}, u32[]{:S(2)}) collective-permute-start(f32[8,128]{1,0:T(8,128)S(1)} %log_add_fusion.1), channel_id=1, source_target_pairs={{0,2},{2,0},{1,3},{3,1},{4,6},{6,4},{5,7},{7,5},{8,10},{10,8},{9,1... | collective-permute-start | bytes 12296 | tf_op jit(solution)/shard_map/ppermute | solution.py:526
